TPU v7x, 128 devices: a whole 4x4x4 slice. The times are simulated.
128 devices in a mesh: seq: 2 (over core), expert: 8 (over z_hi, x), tensor: 8 (over y, z_lo).
Axes of the slice: x: 4, y: 4, z: 4 (z_hi: 2, z_lo: 2; z = z_hi * 2 + z_lo), core: 2. Of those that a mesh axis runs over, the one named last changes fastest.
Arguments:
- tokens: bfloat16 [2048, 4096], P(('seq', 'expert'), 'tensor'), may hold values from -100 to 100
- routes: int32 [2048, 2], P(('seq', 'expert')), may hold values from 0 to 7, all different within a row; in each aligned block of 128 rows (0 to 127, 128 to 255, ...) at most 64 rows name the same one
- route_weights: float32 [2048, 2], P(('seq', 'expert')), may hold values from 0.1 to 0.9
- norm_gain: float32 [4096], P('tensor'), may hold values from 0.1 to 1.9
- final_gain: float32 [4096], P('tensor'), may hold values from 0.1 to 1.9
- w_gate: bfloat16 [8, 4096, 14336], P('expert', None, ('seq', 'tensor')), may hold values from -0.09375 to 0.09375
- w_up: bfloat16 [8, 4096, 14336], P('expert', None, ('seq', 'tensor')), may hold values from -0.09375 to 0.09375
- w_down: bfloat16 [8, 14336, 4096], P('expert', ('seq', 'tensor')), may hold values from -0.09375 to 0.09375
- head_weight: bfloat16 [4096, 32000], P(None, ('expert', 'tensor')), may hold values from -100 to 100
- targets: int32 [2048], P('seq'), may hold values from 0 to 31999
Outputs:
- loss: float32 [2048], P(('seq', 'expert', 'tensor'))
Inputs may be any that keep to these rules, and one draw needn't show every extreme that they name: Within each aligned block of 128 rows no expert is named by more than 64 routes, a bound that some block reaches; the two experts of a row differ.
All inputs are finite; a program needn't handle non-finite values.
Results may differ from a plain program's by a relative error of at most 0.00365.
Values may be sent and summed in bfloat16 or wider, within the bound.
A program may use at most 192 MiB of HBM per device.

v0:
```python
import jax
import jax.numpy as jnp
from jax import lax
from jax.sharding import PartitionSpec as P

epsilon = 1e-05


def joined(part, axis, combine):
    gathered = jax.tree.map(lambda a: lax.all_gather(a, axis), part)

    def take(source):
        return jax.tree.map(lambda a: lax.dynamic_index_in_dim(a, source, 0, False), gathered)

    return lax.fori_loop(
        1, lax.axis_size(axis), lambda source, state: combine(state, take(source)), take(0)
    )


def combine_totals(left_terms, right_terms):
    row_top = jnp.maximum(left_terms[0], right_terms[0])
    row_total = left_terms[1] * jnp.exp(left_terms[0] - row_top) + right_terms[1] * jnp.exp(
        right_terms[0] - row_top
    )
    return (row_top, row_total, left_terms[2] + right_terms[2])


def on_device(
    tokens, routes, route_weights, norm_gain, final_gain, w_gate, w_up, w_down, head_weight, targets
):
    tok_rows, slice_width = tokens.shape
    n_seq = lax.axis_size("seq")
    n_expert = lax.axis_size("expert")
    n_tensor = lax.axis_size("tensor")
    full_width = slice_width * n_tensor
    experts = w_gate.shape[0] * n_expert
    capacity = 4 * tok_rows // experts
    slots_all = experts * capacity
    hidden_part = w_gate.shape[2]
    vocab_part = head_weight.shape[1]
    token_float = tokens.astype(jnp.float32)
    first_squares = lax.psum(jnp.sum(token_float * token_float, axis=1), "tensor")
    normed = (
        token_float * lax.rsqrt(first_squares / full_width + epsilon)[:, None] * norm_gain[None, :]
    ).astype(jnp.bfloat16)
    expert_ids = jnp.arange(experts, dtype=jnp.int32)
    onehot = (routes.reshape(-1)[:, None] == expert_ids[None, :]).astype(jnp.int32)
    earlier = jnp.cumsum(onehot, axis=0) - onehot
    slot_index = jnp.sum(earlier * onehot, axis=1).reshape(tok_rows, 2)
    place_index = routes * capacity + slot_index
    positions = jnp.arange(slots_all, dtype=jnp.int32)
    first_hit = place_index[None, :, 0] == positions[:, None]
    second_hit = place_index[None, :, 1] == positions[:, None]
    dispatch = (first_hit | second_hit).astype(jnp.bfloat16)
    outgoing = (
        jnp.dot(dispatch, normed, preferred_element_type=jnp.float32)
        .astype(jnp.bfloat16)
        .reshape(experts, capacity, slice_width)
    )
    incoming = lax.all_to_all(outgoing, "expert", split_axis=0, concat_axis=0, tiled=True)
    gate_local = w_gate[0]
    up_local = w_up[0]
    down_local = w_down[0]
    zero_acc = jnp.zeros((n_seq, slots_all, hidden_part), jnp.float32)

    def add_rows(carry_in, row_block, seq_index, row_start):
        gate_rows = lax.dynamic_slice_in_dim(gate_local, row_start, row_block.shape[1], 0)
        up_rows = lax.dynamic_slice_in_dim(up_local, row_start, row_block.shape[1], 0)
        gate_part = jnp.dot(row_block, gate_rows, preferred_element_type=jnp.float32)
        up_part = jnp.dot(row_block, up_rows, preferred_element_type=jnp.float32)
        gate_acc = lax.dynamic_update_index_in_dim(
            carry_in[0],
            lax.dynamic_index_in_dim(carry_in[0], seq_index, 0, False) + gate_part,
            seq_index,
            0,
        )
        up_acc = lax.dynamic_update_index_in_dim(
            carry_in[1],
            lax.dynamic_index_in_dim(carry_in[1], seq_index, 0, False) + up_part,
            seq_index,
            0,
        )
        return (gate_acc, up_acc)

    shard_piece = lax.all_gather(incoming[None], ("seq", "tensor"), axis=0, tiled=True)

    def add_piece(step_index, running):
        row_block = lax.dynamic_index_in_dim(shard_piece, step_index, 0, False).reshape(
            slots_all, slice_width
        )
        return add_rows(
            running, row_block, step_index // n_tensor, step_index % n_tensor * slice_width
        )

    gate_sum, up_sum = lax.fori_loop(0, shard_piece.shape[0], add_piece, (zero_acc, zero_acc))
    hidden = (jax.nn.silu(gate_sum) * up_sum).astype(jnp.bfloat16)

    def one_block(block_index):
        seq_index = block_index // n_tensor
        column_start = block_index % n_tensor * slice_width
        hidden_rows = lax.dynamic_index_in_dim(hidden, seq_index, 0, False)
        down_cols = lax.dynamic_slice_in_dim(down_local, column_start, slice_width, 1)
        return jnp.dot(hidden_rows, down_cols, preferred_element_type=jnp.float32)

    blocks = lax.map(
        one_block,
        jnp.arange(lax.axis_size(("seq", "tensor")) * slots_all // slots_all, dtype=jnp.int32),
    )
    expert_out = lax.psum_scatter(
        blocks.reshape(lax.axis_size(("seq", "tensor")) * slots_all, slice_width),
        ("seq", "tensor"),
        scatter_dimension=0,
        tiled=True,
    )
    outgoing_back = expert_out.astype(jnp.bfloat16).reshape(experts, capacity, slice_width)
    returned = lax.all_to_all(outgoing_back, "expert", split_axis=0, concat_axis=0, tiled=True)
    combine_matrix = route_weights[:, 0:1] * (place_index[:, 0:1] == positions[None, :]).astype(
        jnp.float32
    )
    combine_matrix = combine_matrix + route_weights[:, 1:2] * (
        place_index[:, 1:2] == positions[None, :]
    ).astype(jnp.float32)
    mixed_rows = jnp.dot(
        combine_matrix,
        returned.reshape(slots_all, slice_width).astype(jnp.float32),
        precision=lax.Precision.HIGHEST,
    )
    residual = (token_float + mixed_rows).astype(jnp.bfloat16)
    residual_float = residual.astype(jnp.float32)
    second_squares = lax.psum(jnp.sum(residual_float * residual_float, axis=1), "tensor")
    final_rows = (
        residual_float
        * lax.rsqrt(second_squares / full_width + epsilon)[:, None]
        * final_gain[None, :]
    ).astype(jnp.bfloat16)
    zero_logits = jnp.zeros((n_expert, tok_rows, vocab_part), jnp.float32)
    fold_shard_piece = lax.all_gather(final_rows[None], ("expert", "tensor"), axis=0, tiled=True)

    def add_piece(step_index, running):
        expert_index = step_index // n_tensor
        row_start = step_index % n_tensor * slice_width
        row_block = lax.dynamic_index_in_dim(fold_shard_piece, step_index, 0, False)
        head_rows = lax.dynamic_slice_in_dim(head_weight, row_start, slice_width, 0)
        partial_logits = jnp.dot(row_block, head_rows, preferred_element_type=jnp.float32)
        return lax.dynamic_update_index_in_dim(
            running,
            lax.dynamic_index_in_dim(running, expert_index, 0, False) + partial_logits,
            expert_index,
            0,
        )

    logits = lax.fori_loop(0, fold_shard_piece.shape[0], add_piece, zero_logits)
    logits = logits.reshape(n_expert * tok_rows, vocab_part)
    vocab_start = (lax.axis_index("expert") * n_tensor + lax.axis_index("tensor")) * vocab_part
    local_top = jnp.max(logits, axis=1)
    local_total = jnp.sum(jnp.exp(logits - local_top[:, None]), axis=1)
    target_hit = targets[:, None] - vocab_start == jnp.arange(vocab_part, dtype=jnp.int32)[None, :]
    target_logit = jnp.sum(jnp.where(target_hit, logits, jnp.zeros_like(logits)), axis=1)
    own_rows = tok_rows // n_tensor
    row_top, row_total, row_target = joined(
        (local_top, local_total, target_logit), ("expert", "tensor"), combine_totals
    )
    loss_all = row_top + jnp.log(row_total) - row_target
    own_start = lax.axis_index("expert") * tok_rows + lax.axis_index("tensor") * own_rows
    return lax.dynamic_slice_in_dim(loss_all, own_start, own_rows)


def solution(mesh):
    return jax.shard_map(
        on_device,
        mesh=mesh,
        in_specs=(
            P(("seq", "expert"), "tensor"),
            P(("seq", "expert"), None),
            P(("seq", "expert"), None),
            P("tensor"),
            P("tensor"),
            P("expert", None, ("seq", "tensor")),
            P("expert", None, ("seq", "tensor")),
            P("expert", ("seq", "tensor"), None),
            P(None, ("expert", "tensor")),
            P("seq"),
        ),
        out_specs=P(("seq", "expert", "tensor")),
        check_vma=False,
    )
```

profile of v0, /device:TPU:0, one launch (start us, length us, event | category | flops | bytes accessed | tf_op | source)
XLA Modules:
  0.0 1736.7 jit_solution(6503815043042770772)
XLA Ops:
  10.5 20.4 %psum.14 = f32[128]{0:T(128)S(1)} all-reduce(f32[128]{0:T(128)S(1)} %fusion.17), channel_id=1, replica_groups=mesh['seq'=2,'expert'=8,'tensor'=8] {'tensor'}, use_global_device_ids=true, to_apply=%region_4.5 | all-reduce | flops 128 | bytes 1024 | tf_op jit(solution)/shard_map/psum | solution.py:42
  32.2 17.4 %all_to_all.10 = bf16[8,64,512]{2,1,0:T(8,128)(2,1)} all-to-all(bf16[8,64,512]{2,1,0:T(8,128)(2,1)S(1)} %bitcast.115), channel_id=1, replica_groups=mesh['seq'=2,'expert'=8,'tensor'=8] {'expert'}, dimensions={0} | all-to-all | bytes 1048576 | tf_op jit(solution)/shard_map/all_to_all | solution.py:60
  49.7 46.9 %all-gather.8.cloned.1.call-done = bf16[128,64,512]{2,1,0:T(8,128)(2,1)} async-done(((bf16[8,64,512]{2,1,0:T(8,128)(2,1)}), bf16[128,64,512]{2,1,0:T(8,128)(2,1)}) %all-gather.8.cloned.1.call-update) | async-done | bytes 8388624 | tf_op jit(solution)/shard_map/all_gather | solution.py:85
  100.8 185.3 %while.63 = (s32[]{:T(128)}, f32[2,512,896]{2,1,0:T(8,128)}, f32[2,512,896]{2,1,0:T(8,128)}, bf16[16,8,64,512]{3,2,1,0:T(8,128)(2,1)}, bf16[4096,896]{1,0:T(8,12...) while((s32[]{:T(128)}, f32[2,512,896]{2,1,0:T(8,128)}, ...), condition=%wide.region_6.7_spmd, body=%wide.region_5.6_spmd.sunk | while | flops 940441600 | bytes 18612584 | solution.py:95
  100.8 3.6 constant_dynamic-slice_fusion.12
  105.5 3.8 bitcast_dynamic-update-slice_fusion.5
  109.3 3.2 bitcast_dynamic-update-slice_fusion.4
  112.5 3.6 constant_dynamic-slice_fusion.12
  117.2 3.8 bitcast_dynamic-update-slice_fusion.5
  121.0 3.2 bitcast_dynamic-update-slice_fusion.4
  124.2 3.6 constant_dynamic-slice_fusion.12
  128.8 3.8 bitcast_dynamic-update-slice_fusion.5
  132.7 3.2 bitcast_dynamic-update-slice_fusion.4
  135.9 3.6 constant_dynamic-slice_fusion.12
  140.5 3.8 bitcast_dynamic-update-slice_fusion.5
  144.4 3.2 bitcast_dynamic-update-slice_fusion.4
  147.6 3.6 constant_dynamic-slice_fusion.12
  152.2 3.8 bitcast_dynamic-update-slice_fusion.5
  156.0 3.2 bitcast_dynamic-update-slice_fusion.4
  159.2 3.6 constant_dynamic-slice_fusion.12
  163.9 3.8 bitcast_dynamic-update-slice_fusion.5
  167.7 3.2 bitcast_dynamic-update-slice_fusion.4
  170.9 3.6 constant_dynamic-slice_fusion.12
  175.6 3.8 bitcast_dynamic-update-slice_fusion.5
  179.4 3.2 bitcast_dynamic-update-slice_fusion.4
  182.6 3.6 constant_dynamic-slice_fusion.12
  187.2 3.8 bitcast_dynamic-update-slice_fusion.5
  191.1 3.2 bitcast_dynamic-update-slice_fusion.4
  194.3 3.6 constant_dynamic-slice_fusion.12
  198.9 3.7 bitcast_dynamic-update-slice_fusion.5
  202.7 3.1 bitcast_dynamic-update-slice_fusion.4
  205.8 3.6 constant_dynamic-slice_fusion.12
  210.4 3.7 bitcast_dynamic-update-slice_fusion.5
  214.1 3.1 bitcast_dynamic-update-slice_fusion.4
  217.2 3.6 constant_dynamic-slice_fusion.12
  221.9 3.7 bitcast_dynamic-update-slice_fusion.5
  225.6 3.1 bitcast_dynamic-update-slice_fusion.4
  228.7 3.6 constant_dynamic-slice_fusion.12
  233.4 3.7 bitcast_dynamic-update-slice_fusion.5
  237.1 3.1 bitcast_dynamic-update-slice_fusion.4
  240.2 3.6 constant_dynamic-slice_fusion.12
  244.9 3.7 bitcast_dynamic-update-slice_fusion.5
  248.6 3.1 bitcast_dynamic-update-slice_fusion.4
  251.7 3.6 constant_dynamic-slice_fusion.12
  256.3 3.7 bitcast_dynamic-update-slice_fusion.5
  260.1 3.1 bitcast_dynamic-update-slice_fusion.4
  263.2 3.6 constant_dynamic-slice_fusion.12
  267.8 3.7 bitcast_dynamic-update-slice_fusion.5
  271.5 3.1 bitcast_dynamic-update-slice_fusion.4
  274.7 3.6 constant_dynamic-slice_fusion.12
  279.3 3.7 bitcast_dynamic-update-slice_fusion.5
  283.0 3.1 bitcast_dynamic-update-slice_fusion.4
  286.1 4.1 multiply_convert_fusion
  290.3 92.1 %while.64 = (s32[]{:T(128)}, f32[16,512,512]{2,1,0:T(8,128)}, s32[16]{0:T(128)S(1)}, bf16[2,512,896]{2,1,0:T(8,128)(2,1)S(1)}, bf16[896,4096]{1,0:T(8,128)(2,1)}...) while((s32[]{:T(128)}, f32[16,512,512]{2,1,0:T(8,128)}, ...), condition=%wide.region_8.9_spmd, body=%wide.region_7.8_spmd.sunk | while | flops 469762080 | bytes 2884516 | solution.py:105
  382.4 350.0 %reduce-scatter.2.cloned.1.call-done = f32[512,512]{1,0:T(8,128)} async-done(((f32[8192,512]{1,0:T(8,128)}), f32[512,512]{1,0:T(8,128)}) %reduce-scatter.2.cloned.1.call-update) | async-done | bytes 1048592 | tf_op jit(solution)/shard_map/reduce_scatter | solution.py:109
  734.5 6.6 all-to-all-start.1
  741.1 11.4 all-to-all-done.1
  753.1 18.6 %psum.15 = f32[128]{0:T(128)S(1)} all-reduce(f32[128]{0:T(128)S(1)} %get-tuple-element.585), channel_id=1, replica_groups=mesh['seq'=2,'expert'=8,'tensor'=8] {'tensor'}, use_global_device_ids=true, to_apply=%region_11.12 | all-reduce | flops 128 | bytes 1024 | tf_op jit(solution)/shard_map/psum | solution.py:130
  772.4 336.7 %all-gather.10.cloned.1.call-done = bf16[8192,512]{1,0:T(8,128)(2,1)} async-done(((bf16[128,512]{1,0:T(8,128)(2,1)}), bf16[8192,512]{1,0:T(8,128)(2,1)}) %all-gather.10.cloned.1.call-update) | async-done | bytes 8388624 | tf_op jit(solution)/shard_map/all_gather | solution.py:137
  1109.3 94.9 %while.65 = (s32[]{:T(128)}, f32[8,128,500]{1,2,0:T(8,128)S(1)}, bf16[64,128,512]{2,1,0:T(8,128)(2,1)}, bf16[4096,500]{0,1:T(8,128)(2,1)}, s32[]{:T(128)}, /*ind...) while((s32[]{:T(128)}, f32[8,128,500]{1,2,0:T(8,128)S(1)}, ...), condition=%wide.region_13.14_spmd, body=%wide.region_12.13_spmd.sunk | while | flops 65600020 | bytes 1676100 | solution.py:152
  1204.8 175.6 %all-gather.3 = f32[64,1,1024]{2,1,0:T(1,128)S(1)} all-gather(f32[1,1,1024]{2,1,0:T(1,128)S(1)} %bitcast.130), channel_id=1, replica_groups=mesh['seq'=2,'expert'=8,'tensor'=8] {'expert','tensor'}, dimensions={0}, use_global_device_ids=true | all-gather | bytes 266240 | tf_op jit(solution)/shard_map/all_gather | solution.py:10
  1380.4 170.6 %all-gather.4 = f32[64,1,1024]{2,1,0:T(1,128)S(1)} all-gather(f32[1,1,1024]{2,1,0:T(1,128)S(1)} %bitcast.129), channel_id=1, replica_groups=mesh['seq'=2,'expert'=8,'tensor'=8] {'expert','tensor'}, dimensions={0}, use_global_device_ids=true | all-gather | bytes 266240 | tf_op jit(solution)/shard_map/all_gather | solution.py:10
  1551.0 172.6 %all-gather.2 = f32[64,1,1024]{2,1,0:T(1,128)S(1)} all-gather(f32[1,1,1024]{2,1,0:T(1,128)S(1)} %bitcast.128), channel_id=1, replica_groups=mesh['seq'=2,'expert'=8,'tensor'=8] {'expert','tensor'}, dimensions={0}, use_global_device_ids=true | all-gather | bytes 266240 | tf_op jit(solution)/shard_map/all_gather | solution.py:10
  1723.7 5.9 while.66
  (479 shorter events, 181.9 us)
Async XLA Ops:
  6.5 90.1 %all-gather.8.cloned.1.call-start = ((), (), s32[]{:S(2)}) async-start(), calls=%async_computation.4 | async-start | bytes 8912896 | tf_op jit(solution)/shard_map/all_gather | solution.py:85
  49.7 682.7 %reduce-scatter.2.cloned.1.call-start = ((), (), s32[]{:S(2)}) async-start(), calls=%async_computation.3 | async-start | bytes 17825792 | tf_op jit(solution)/shard_map/reduce_scatter | solution.py:109
  382.4 358.7 %copy-start.3 = (f32[128,2]{0,1:T(2,128)S(1)}, f32[128,2]{0,1:T(2,128)}, u32[]{:S(2)}) copy-start(f32[128,2]{0,1:T(2,128)} %param.20) | copy-start | bytes 3076
  382.4 370.2 %copy-start = (bf16[128,512]{1,0:T(8,128)(2,1)S(1)}, bf16[128,512]{1,0:T(8,128)(2,1)}, u32[]{:S(2)}) copy-start(bf16[128,512]{1,0:T(8,128)(2,1)} %param.18) | copy-start | bytes 393220
  382.4 389.2 %copy-start.2 = (f32[512]{0:T(512)S(1)}, f32[512]{0:T(512)}, u32[]{:S(2)}) copy-start(f32[512]{0:T(512)} %param.22) | copy-start | bytes 6148
  382.4 390.0 %copy-start.1 = (s32[1024]{0:T(1024)S(1)}, s32[1024]{0:T(1024)}, u32[]{:S(2)}) copy-start(s32[1024]{0:T(1024)} %param.27) | copy-start | bytes 12292
  734.5 18.1 %all-to-all-start.1 = ((bf16[8,64,512]{2,1,0:T(8,128)(2,1)}), bf16[8,64,512]{2,1,0:T(8,128)(2,1)S(1)}, u32[]{:S(2)}, u32[]{:S(2)}) async-start(bf16[8,64,512]{2,1,0:T(8,128)(2,1)} %bitcast.26), calls=%async_computation.2 | async-start | bytes 1048576 | tf_op jit(solution)/shard_map/all_to_all | solution.py:116
  741.0 368.1 %all-gather.10.cloned.1.call-start = ((), (), s32[]{:S(2)}) async-start(), calls=%async_computation.5 | async-start | bytes 8519680 | tf_op jit(solution)/shard_map/all_gather | solution.py:137
Sparse Core Ops, SparseCore 0:
  49.8 46.7 all-gather.7
  382.5 349.8 reduce-scatter.1
  772.5 336.5 all-gather.9
where the time goes:
time: 1740 us
  waiting for transfers between devices  745 us (43%)
  blocking collectives  575 us (33%)
  matrix products  249 us (14%)
  local copies, waits for them, and re-layouts  93.4 us (5%)
  loops' own time  42.9 us (2%)
    all_gather x3, blocking collectives, joined(): gathered = jax.tree.map(lambda a: lax.all_gather(a, axis), part)  519 us
    reduce_scatter x1, waiting for transfers between devices, on_device(): lax.psum_scatter(blocks.reshape(lax.axis_size(('seq', 'tensor')) * slots_...  350 us
    all_gather x1, waiting for transfers between devices, on_device(): lax.all_gather(final_rows[None], ('expert', 'tensor'), axis=0, tiled=True)  337 us
    dot_general x64, matrix products, add_piece(): jnp.dot(row_block, head_rows, preferred_element_type=jnp.float32)  90.2 us
    dot_general x16, matrix products, add_rows(): up_part = jnp.dot(row_block, up_rows, preferred_element_type=jnp.float32)  60.5 us
    dynamic_slice x16, local copies, waits for them, and re-layouts, add_rows(): lax.dynamic_index_in_dim(carry_in[1], seq_index, 0, False) + up_part  56.8 us
    dot_general x16, matrix products, add_rows(): jnp.dot(row_block, gate_rows, preferred_element_type=jnp.float32)  50.5 us
    all_gather x1, waiting for transfers between devices, on_device(): lax.all_gather(incoming[None], ('seq', 'tensor'), axis=0, tiled=True)  46.9 us
  transfers between devices with their start and end apart: 4, of which 4 were waited for; matrix products, arithmetic and copies ran while one was open for 0% of the time, Pallas kernels for 0%

commit v1 on v0

v1 whole, which is shorter than its diff:
```python
import jax
import jax.numpy as jnp
from jax import lax
from jax.sharding import PartitionSpec as P

epsilon = 1e-05


def merge_terms(stacked):
    top = jnp.max(stacked[:, 0], axis=0)
    total = jnp.sum(stacked[:, 1] * jnp.exp(stacked[:, 0] - top[None]), axis=0)
    return jnp.stack([top, total, jnp.sum(stacked[:, 2], axis=0)])


def on_device(
    tokens, routes, route_weights, norm_gain, final_gain, w_gate, w_up, w_down, head_weight, targets
):
    tok_rows, slice_width = tokens.shape
    n_seq = lax.axis_size("seq")
    n_expert = lax.axis_size("expert")
    n_tensor = lax.axis_size("tensor")
    full_width = slice_width * n_tensor
    experts = w_gate.shape[0] * n_expert
    capacity = 4 * tok_rows // experts
    slots_all = experts * capacity
    vocab_part = head_weight.shape[1]
    token_float = tokens.astype(jnp.float32)
    first_squares = lax.psum(jnp.sum(token_float * token_float, axis=1), "tensor")
    normed = (
        token_float * lax.rsqrt(first_squares / full_width + epsilon)[:, None] * norm_gain[None, :]
    ).astype(jnp.bfloat16)
    expert_ids = jnp.arange(experts, dtype=jnp.int32)
    onehot = (routes.reshape(-1)[:, None] == expert_ids[None, :]).astype(jnp.int32)
    earlier = jnp.cumsum(onehot, axis=0) - onehot
    slot_index = jnp.sum(earlier * onehot, axis=1).reshape(tok_rows, 2)
    place_index = routes * capacity + slot_index
    positions = jnp.arange(slots_all, dtype=jnp.int32)
    first_hit = place_index[None, :, 0] == positions[:, None]
    second_hit = place_index[None, :, 1] == positions[:, None]
    dispatch = (first_hit | second_hit).astype(jnp.bfloat16)
    outgoing = (
        jnp.dot(dispatch, normed, preferred_element_type=jnp.float32)
        .astype(jnp.bfloat16)
        .reshape(experts, capacity, slice_width)
    )
    incoming = lax.all_to_all(outgoing, "expert", split_axis=0, concat_axis=0, tiled=True)
    pieces = lax.all_gather(incoming[None], ("seq", "tensor"), axis=0, tiled=True)
    rows = (
        pieces.reshape(n_seq, n_tensor, slots_all, slice_width)
        .transpose(0, 2, 1, 3)
        .reshape(n_seq * slots_all, full_width)
    )
    gate = jnp.dot(rows, w_gate[0], preferred_element_type=jnp.float32)
    up = jnp.dot(rows, w_up[0], preferred_element_type=jnp.float32)
    hidden = (jax.nn.silu(gate) * up).astype(jnp.bfloat16)
    partial = jnp.dot(hidden, w_down[0], preferred_element_type=jnp.float32).astype(jnp.bfloat16)
    blocks = (
        partial.reshape(n_seq, slots_all, n_tensor, slice_width)
        .transpose(0, 2, 1, 3)
        .reshape(n_seq * n_tensor * slots_all, slice_width)
    )
    expert_out = lax.psum_scatter(blocks, ("seq", "tensor"), scatter_dimension=0, tiled=True)
    outgoing_back = expert_out.astype(jnp.bfloat16).reshape(experts, capacity, slice_width)
    returned = lax.all_to_all(outgoing_back, "expert", split_axis=0, concat_axis=0, tiled=True)
    combine_matrix = route_weights[:, 0:1] * (place_index[:, 0:1] == positions[None, :]).astype(
        jnp.float32
    )
    combine_matrix = combine_matrix + route_weights[:, 1:2] * (
        place_index[:, 1:2] == positions[None, :]
    ).astype(jnp.float32)
    mixed_rows = jnp.dot(
        combine_matrix,
        returned.reshape(slots_all, slice_width).astype(jnp.float32),
        precision=lax.Precision.HIGHEST,
    )
    residual = (token_float + mixed_rows).astype(jnp.bfloat16)
    residual_float = residual.astype(jnp.float32)
    second_squares = lax.psum(jnp.sum(residual_float * residual_float, axis=1), "tensor")
    final_rows = (
        residual_float
        * lax.rsqrt(second_squares / full_width + epsilon)[:, None]
        * final_gain[None, :]
    ).astype(jnp.bfloat16)
    final_pieces = lax.all_gather(final_rows[None], ("expert", "tensor"), axis=0, tiled=True)
    all_rows = (
        final_pieces.reshape(n_expert, n_tensor, tok_rows, slice_width)
        .transpose(0, 2, 1, 3)
        .reshape(n_expert * tok_rows, full_width)
    )
    logits = jnp.dot(all_rows, head_weight, preferred_element_type=jnp.float32)
    vocab_start = (lax.axis_index("expert") * n_tensor + lax.axis_index("tensor")) * vocab_part
    local_top = jnp.max(logits, axis=1)
    local_total = jnp.sum(jnp.exp(logits - local_top[:, None]), axis=1)
    target_hit = targets[:, None] - vocab_start == jnp.arange(vocab_part, dtype=jnp.int32)[None, :]
    target_logit = jnp.sum(jnp.where(target_hit, logits, jnp.zeros_like(logits)), axis=1)
    own_rows = tok_rows // n_tensor
    terms = jnp.stack([local_top, local_total, target_logit])
    terms = merge_terms(lax.all_gather(terms, "expert"))
    terms = lax.dynamic_slice_in_dim(terms, lax.axis_index("expert") * tok_rows, tok_rows, 1)
    terms = merge_terms(lax.all_gather(terms, "tensor"))
    loss_all = terms[0] + jnp.log(terms[1]) - terms[2]
    return lax.dynamic_slice_in_dim(loss_all, lax.axis_index("tensor") * own_rows, own_rows)


def solution(mesh):
    return jax.shard_map(
        on_device,
        mesh=mesh,
        in_specs=(
            P(("seq", "expert"), "tensor"),
            P(("seq", "expert"), None),
            P(("seq", "expert"), None),
            P("tensor"),
            P("tensor"),
            P("expert", None, ("seq", "tensor")),
            P("expert", None, ("seq", "tensor")),
            P("expert", ("seq", "tensor"), None),
            P(None, ("expert", "tensor")),
            P("seq"),
        ),
        out_specs=P(("seq", "expert", "tensor")),
        check_vma=False,
    )
```

time: 1740 us -> 839 us (0.48)
  blocking collectives: 575 us -> 115 us
  matrix products: 249 us -> 43.3 us
  waiting for transfers between devices: 745 us -> 577 us
  loops' own time: 42.9 us -> 0 us
  local copies, waits for them, and re-layouts: 93.4 us -> 71.5 us
    all_gather x3 -> x2, blocking collectives: 519 us -> 57.9 us  [the longest x1 34.2 us: on_device(): terms = merge_terms(lax.all_gather(terms, 'expert'))]
    dot_general x112 -> x4, matrix products: 247 us -> 41.5 us  [the longest x1 12.7 us: on_device(): up = jnp.dot(rows, w_up[0], preferred_element_type=jnp.float32)]
    reduce_scatter x1, waiting for transfers between devices: 350 us -> 181 us  [on_device(): lax.psum_scatter(blocks, ('seq', 'tensor'), scatter_dimension=0, tiled=True)]
    dynamic_slice x242 -> x1, local copies, waits for them, and re-layouts: 87.4 us -> 0.59 us  [on_device(): lax.dynamic_slice_in_dim(loss_all, lax.axis_index('tensor') * own_rows, o...]
    another operation x4 -> x0, loops' own time: 42.9 us -> none  [the longest x1 36.5 us: on_device(): lax.map(one_block, jnp.arange(lax.axis_size(('seq', 'tensor')) * slots_al...]
    unnamed x12 -> x22, local copies, waits for them, and re-layouts: 0.95 us -> 37.6 us
    reshape x0 -> x2, local copies, waits for them, and re-layouts: none -> 21.3 us  [the longest x1 11.7 us: on_device(): final_pieces.reshape(n_expert, n_tensor, tok_rows, slice_width)]
where the time goes in v1:
time: 839 us; the launch traced here: 830 us
  waiting for transfers between devices  577 us (69%)
  blocking collectives  115 us (14%)
  local copies, waits for them, and re-layouts  71.5 us (9%)
  matrix products  43.3 us (5%)
  between operations  13.8 us (2%)
    all_gather x1, waiting for transfers between devices, on_device(): lax.all_gather(final_rows[None], ('expert', 'tensor'), axis=0, tiled=True)  337 us
    reduce_scatter x1, waiting for transfers between devices, on_device(): lax.psum_scatter(blocks, ('seq', 'tensor'), scatter_dimension=0, tiled=True)  181 us
    all_gather x1, waiting for transfers between devices, on_device(): lax.all_gather(incoming[None], ('seq', 'tensor'), axis=0, tiled=True)  46.9 us
    unnamed x22, local copies, waits for them, and re-layouts  37.6 us
    all_gather x1, blocking collectives, on_device(): terms = merge_terms(lax.all_gather(terms, 'expert'))  34.2 us
    all_gather x1, blocking collectives, on_device(): terms = merge_terms(lax.all_gather(terms, 'tensor'))  23.8 us
    psum x1, blocking collectives, on_device(): lax.psum(jnp.sum(token_float * token_float, axis=1), 'tensor')  20.4 us
    psum x1, blocking collectives, on_device(): lax.psum(jnp.sum(residual_float * residual_float, axis=1), 'tensor')  18.8 us
  transfers between devices with their start and end apart: 4, of which 4 were waited for; matrix products, arithmetic and copies ran while one was open for 0% of the time, Pallas kernels for 0%

profile of v1, /device:TPU:0, one launch (start us, length us, event | category | flops | bytes accessed | tf_op | source)
XLA Modules:
  0.0 830.3 jit_solution(3532746267100013564)
XLA Ops:
  6.5 0.0 all-gather.9.cloned.1.call-start
  6.5 0.8 copy.39
  7.3 0.1 eq.98
  7.5 0.1 eq.94
  7.6 0.6 reduce-window.6
  8.2 0.2 slice_reduce_fusion.1
  8.5 0.1 fusion.32
  8.6 0.1 reshape.59
  8.7 0.1 copy.41
  8.8 0.7 multiply_add_fusion
  9.5 1.0 fusion.9
  10.5 20.4 %psum.14 = f32[128]{0:T(128)S(1)} all-reduce(f32[128]{0:T(128)S(1)} %fusion.9), channel_id=1, replica_groups=mesh['seq'=2,'expert'=8,'tensor'=8] {'tensor'}, use_global_device_ids=true, to_apply=%region_4.5 | all-reduce | flops 128 | bytes 1024 | tf_op jit(solution)/shard_map/psum | solution.py:28
  30.9 1.3 convolution_convert_fusion.1
  32.2 17.4 %all_to_all.10 = bf16[8,64,512]{2,1,0:T(8,128)(2,1)} all-to-all(bf16[8,64,512]{2,1,0:T(8,128)(2,1)S(1)} %bitcast.89), channel_id=1, replica_groups=mesh['seq'=2,'expert'=8,'tensor'=8] {'expert'}, dimensions={0} | all-to-all | bytes 1048576 | tf_op jit(solution)/shard_map/all_to_all | solution.py:46
  49.7 0.0 all-gather.9.cloned.1.call-update
  49.7 0.0 reduce-scatter.2.cloned.1.call-start
  49.7 46.9 %all-gather.9.cloned.1.call-done = bf16[128,64,512]{2,1,0:T(8,128)(2,1)} async-done(((bf16[8,64,512]{2,1,0:T(8,128)(2,1)}), bf16[128,64,512]{2,1,0:T(8,128)(2,1)}) %all-gather.9.cloned.1.call-update) | async-done | bytes 8388624 | tf_op jit(solution)/shard_map/all_gather | solution.py:47
  96.6 11.3 %copy.42 = bf16[2,512,8,512]{3,2,1,0:T(8,128)(2,1)} copy(bf16[2,512,8,512]{3,1,2,0:T(8,128)(2,1)} %bitcast.84) | data formatting | bytes 16777216 | tf_op jit(solution)/shard_map/transpose | solution.py:50
  108.0 0.0 slice-start
  108.0 12.3 %copy.51 = bf16[128,8,8,512]{3,1,2,0:T(8,128)(2,1)} copy(bf16[128,8,8,512]{3,2,1,0:T(8,128)(2,1)} %bitcast.80) | data formatting | bytes 16777216
  120.3 0.0 copy-start
  120.3 0.0 slice-start.1
  120.3 0.0 slice-start.2
  120.3 12.7 %fusion.1 = f32[1024,896]{1,0:T(8,128)S(1)} fusion(bf16[1024,4096]{1,0:T(8,128)(2,1)} %bitcast.86, bf16[1,4096,896]{2,1,0:T(8,128)(2,1)} %param.16), kind=kOutput, calls=%fused_computation.2 | convolution fusion | flops 7516192768 | bytes 19398656 | tf_op jit(solution)/shard_map/dot_general | solution.py:54
  133.0 0.0 slice-done
  133.0 0.0 copy-done
  133.0 0.0 slice-done.1
  133.0 0.0 slice-start.3
  133.1 9.2 %multiply_convert_fusion = bf16[1024,896]{1,0:T(8,128)(2,1)S(1)} fusion(f32[1024,896]{1,0:T(8,128)S(1)} %fusion.1, bf16[1024,4096]{1,0:T(8,128)(2,1)S(1)} %bitcast.87, bf16[1,4096,896]{2,1,0:T(8,128)(2,1)S(1)} %bitcast.102), kind=kOutput, calls=%fused_computation.6 | convolution fusion | flops 7521697792 | bytes 21233664 | tf_op jit(solution)/shard_map/dot_general | solution.py:53
  142.2 0.0 slice-done.2
  142.2 0.0 slice-done.3
  142.2 11.3 %convolution_convert_fusion = bf16[1024,4096]{1,0:T(8,128)(2,1)} fusion(bf16[1024,896]{1,0:T(8,128)(2,1)S(1)} %multiply_convert_fusion, bf16[1,896,4096]{2,1,0:T(8,128)(2,1)S(1)} %bitcast.104), kind=kOutput, calls=%fused_computation | convolution fusion | flops 7520387072 | bytes 17563648 | tf_op jit(solution)/shard_map/dot_general | solution.py:56
  153.5 12.2 %copy.52 = bf16[128,8,8,512]{3,2,1,0:T(8,128)(2,1)} copy(bf16[128,8,8,512]{3,1,2,0:T(8,128)(2,1)} %bitcast.88) | data formatting | bytes 16777216
  165.7 9.6 %copy.43 = bf16[2,512,8,512]{3,1,2,0:T(8,128)(2,1)} copy(bf16[2,512,8,512]{3,2,1,0:T(8,128)(2,1)} %bitcast.81) | data formatting | bytes 16777216 | tf_op jit(solution)/shard_map/reshape | solution.py:58
  175.3 0.0 copy-start.4
  175.3 0.0 copy-start.1
  175.3 0.0 copy-start.3
  175.3 0.0 copy-start.2
  175.3 0.0 reduce-scatter.2.cloned.1.call-update
  175.3 181.2 %reduce-scatter.2.cloned.1.call-done = bf16[512,512]{1,0:T(8,128)(2,1)} async-done(((bf16[8192,512]{1,0:T(8,128)(2,1)}), bf16[512,512]{1,0:T(8,128)(2,1)}) %reduce-scatter.2.cloned.1.call-update) | async-done | bytes 524304 | tf_op jit(solution)/shard_map/reduce_scatter | solution.py:62
  356.5 6.1 all-to-all-start.1
  362.6 0.0 all-gather.11.cloned.1.call-start
  362.6 0.0 copy-done.4
  362.7 12.0 %all-to-all-done.1 = bf16[8,64,512]{2,1,0:T(8,128)(2,1)S(1)} async-done(((bf16[8,64,512]{2,1,0:T(8,128)(2,1)}), bf16[8,64,512]{2,1,0:T(8,128)(2,1)S(1)}, u32[]{:S(2)}, u32[]{:S(2)}) %all-to-all-start.1) | async-done | bytes 524320 | tf_op jit(solution)/shard_map/all_to_all | solution.py:64
  374.7 0.0 copy-done.1
  374.7 0.5 multiply_reduce_fusion
  375.2 18.8 %psum.15 = f32[128]{0:T(128)S(1)} all-reduce(f32[128]{0:T(128)S(1)} %get-tuple-element.20), channel_id=1, replica_groups=mesh['seq'=2,'expert'=8,'tensor'=8] {'tensor'}, use_global_device_ids=true, to_apply=%region_7.8 | all-reduce | flops 128 | bytes 1024 | tf_op jit(solution)/shard_map/psum | solution.py:78
  394.0 0.0 copy-done.3
  394.0 0.8 multiply_convert_fusion.1
  394.7 0.0 all-gather.11.cloned.1.call-update
  394.7 0.0 copy-done.2
  394.8 336.7 %all-gather.11.cloned.1.call-done = bf16[8192,512]{1,0:T(8,128)(2,1)} async-done(((bf16[128,512]{1,0:T(8,128)(2,1)}), bf16[8192,512]{1,0:T(8,128)(2,1)}) %all-gather.11.cloned.1.call-update) | async-done | bytes 8388624 | tf_op jit(solution)/shard_map/all_gather | solution.py:84
  731.5 11.7 %copy.44 = bf16[8,8,128,512]{3,1,2,0:T(8,128)(2,1)} copy(bf16[8,8,128,512]{3,2,1,0:T(8,128)(2,1)} %bitcast.83) | data formatting | bytes 16777216 | tf_op jit(solution)/shard_map/reshape | solution.py:86
  743.2 12.2 %copy.53 = bf16[128,8,8,512]{3,1,2,0:T(8,128)(2,1)} copy(bf16[128,8,8,512]{3,2,1,0:T(8,128)(2,1)} %bitcast.82) | data formatting | bytes 16777216
  755.4 8.4 %fusion.40 = (f32[1024]{0:T(1024)S(1)}, f32[1024,500]{0,1:T(8,128)S(1)}) fusion(bf16[1024,4096]{1,0:T(8,128)(2,1)} %bitcast.85, bf16[4096,500]{0,1:T(8,128)(2,1)} %param.18), kind=kOutput, calls=%fused_computation.73 | convolution fusion | flops 4194814976 | bytes 14536704 | tf_op jit(solution)/shard_map/dot_general | solution.py:90
  763.9 0.5 exponential_reduce_fusion
  764.4 34.2 %all-gather.4 = f32[8,3,1024]{2,1,0:T(4,128)S(1)} all-gather(f32[1,3,1024]{2,1,0:T(4,128)S(1)} %maximum_bitcast_fusion), channel_id=4, replica_groups=mesh['seq'=2,'expert'=8,'tensor'=8] {'expert'}, dimensions={0}, use_global_device_ids=true | all-gather | bytes 110592 | tf_op jit(solution)/shard_map/all_gather | solution.py:98
  798.6 0.1 fusion.38
  798.8 0.1 fusion.36
  798.8 23.8 %all-gather.5 = f32[8,3,128]{2,1,0:T(4,128)S(1)} all-gather(f32[1,3,128]{2,1,0:T(4,128)S(1)} %fusion.36), channel_id=5, replica_groups=mesh['seq'=2,'expert'=8,'tensor'=8] {'tensor'}, dimensions={0}, use_global_device_ids=true | all-gather | bytes 13824 | tf_op jit(solution)/shard_map/all_gather | solution.py:100
  822.7 0.6 dynamic_slice.7
  (16 shorter events, 0.2 us)
Async XLA Ops:
  6.5 90.1 %all-gather.9.cloned.1.call-start = ((), (), s32[]{:S(2)}) async-start(), calls=%async_computation.4 | async-start | bytes 8912896 | tf_op jit(solution)/shard_map/all_gather | solution.py:47
  49.7 306.8 %reduce-scatter.2.cloned.1.call-start = ((), (), s32[]{:S(2)}) async-start(), calls=%async_computation.3 | async-start | bytes 8912896 | tf_op jit(solution)/shard_map/reduce_scatter | solution.py:62
  108.0 25.0 %slice-start = ((s8[7340032]{0:T(1024)(128)(4,1)}), s8[3145728]{0:T(1024)(128)(4,1)S(1)}, s32[]{:S(2)}) async-start(s8[7340032]{0:T(1024)(128)(4,1)} %bitcast.101), calls=%async_computation.6 | async-start | bytes 6291456
  120.3 12.7 %copy-start = (bf16[128,8,8,512]{3,1,2,0:T(8,128)(2,1)S(1)}, bf16[128,8,8,512]{3,1,2,0:T(8,128)(2,1)}, u32[]{:S(2)}) copy-start(bf16[128,8,8,512]{3,1,2,0:T(8,128)(2,1)} %copy.51) | copy-start | bytes 25165828
  120.3 12.7 %slice-start.1 = ((s8[7340032]{0:T(1024)(128)(4,1)}), s8[4194304]{0:T(1024)(128)(4,1)S(1)}, s32[]{:S(2)}) async-start(s8[7340032]{0:T(1024)(128)(4,1)} %bitcast.101), calls=%async_computation.7 | async-start | bytes 8388608
  120.3 21.9 %slice-start.2 = ((s8[7340032]{0:T(1024)(128)(4,1)}), s8[4194304]{0:T(1024)(128)(4,1)S(1)}, s32[]{:S(2)}) async-start(s8[7340032]{0:T(1024)(128)(4,1)} %bitcast.103), calls=%async_computation.8 | async-start | bytes 8388608
  133.0 9.2 %slice-start.3 = ((s8[7340032]{0:T(1024)(128)(4,1)}), s8[3145728]{0:T(1024)(128)(4,1)S(1)}, s32[]{:S(2)}) async-start(s8[7340032]{0:T(1024)(128)(4,1)} %bitcast.103), calls=%async_computation.9 | async-start | bytes 6291456
  175.3 187.3 %copy-start.4 = (f32[128,2]{0,1:T(2,128)S(1)}, f32[128,2]{0,1:T(2,128)}, u32[]{:S(2)}) copy-start(f32[128,2]{0,1:T(2,128)} %param.12) | copy-start | bytes 3076
  175.3 199.4 %copy-start.1 = (bf16[128,512]{1,0:T(8,128)(2,1)S(1)}, bf16[128,512]{1,0:T(8,128)(2,1)}, u32[]{:S(2)}) copy-start(bf16[128,512]{1,0:T(8,128)(2,1)} %param.10) | copy-start | bytes 393220
  175.3 218.6 %copy-start.3 = (f32[512]{0:T(512)S(1)}, f32[512]{0:T(512)}, u32[]{:S(2)}) copy-start(f32[512]{0:T(512)} %param.14) | copy-start | bytes 6148
  175.3 219.4 %copy-start.2 = (s32[1024]{0:T(1024)S(1)}, s32[1024]{0:T(1024)}, u32[]{:S(2)}) copy-start(s32[1024]{0:T(1024)} %param.19) | copy-start | bytes 12292
  356.5 18.1 %all-to-all-start.1 = ((bf16[8,64,512]{2,1,0:T(8,128)(2,1)}), bf16[8,64,512]{2,1,0:T(8,128)(2,1)S(1)}, u32[]{:S(2)}, u32[]{:S(2)}) async-start(bf16[8,64,512]{2,1,0:T(8,128)(2,1)} %bitcast.91), calls=%async_computation.2 | async-start | bytes 1048576 | tf_op jit(solution)/shard_map/all_to_all | solution.py:64
  362.6 368.9 %all-gather.11.cloned.1.call-start = ((), (), s32[]{:S(2)}) async-start(), calls=%async_computation.5 | async-start | bytes 8519680 | tf_op jit(solution)/shard_map/all_gather | solution.py:84
Sparse Core Ops, SparseCore 0:
  49.8 46.7 all-gather.8
  175.5 181.0 reduce-scatter.1
  394.9 336.5 all-gather.10

commit v2 on v1

--- a/solution.py
+++ b/solution.py
@@ -1,15 +1,212 @@
+import functools
 import jax
 import jax.numpy as jnp
 from jax import lax
+from jax.experimental import pallas as pl
+from jax.experimental.pallas import tpu as pltpu
 from jax.sharding import PartitionSpec as P
 
 epsilon = 1e-05
-
-
-def merge_terms(stacked):
-    top = jnp.max(stacked[:, 0], axis=0)
-    total = jnp.sum(stacked[:, 1] * jnp.exp(stacked[:, 0] - top[None]), axis=0)
-    return jnp.stack([top, total, jnp.sum(stacked[:, 2], axis=0)])
+MESH = pl.DeviceIdType.MESH
+COLOR_ROWS = ((0, 48), (48, 48), (96, 32))
+AXES = "xyz"
+
+
+def place():
+    e = lax.axis_index("expert")
+    t = lax.axis_index("tensor")
+    return {"x": e % 4, "y": t // 2, "z": (e // 4) * 2 + t % 2}
+
+
+def device_at(pos):
+    z = pos["z"]
+    return (lax.axis_index("seq"), (z // 2) * 4 + pos["x"], pos["y"] * 2 + z % 2)
+
+
+def moved(pos, axis, by):
+    out = dict(pos)
+    out[axis] = (pos[axis] + by + 4) % 4
+    return out
+
+
+def tensor_peer(k):
+    return (lax.axis_index("seq"), lax.axis_index("expert"), (lax.axis_index("tensor") + k) % 8)
+
+
+def expert_peer(k):
+    return (lax.axis_index("seq"), (lax.axis_index("expert") + k) % 8, lax.axis_index("tensor"))
+
+
+def remote(src, dst, send, recv, dev):
+    return pltpu.make_async_remote_copy(
+        src_ref=src, dst_ref=dst, send_sem=send, recv_sem=recv, device_id=dev, device_id_type=MESH
+    )
+
+
+def greet(peers):
+    barrier = pltpu.get_barrier_semaphore()
+    for dev in peers:
+        pl.semaphore_signal(barrier, inc=1, device_id=dev, device_id_type=MESH)
+    pl.semaphore_wait(barrier, len(peers))
+
+
+def region(buf, full, pos, rows, cols):
+    z = pos["z"]
+    zh = pl.ds(0, 2) if "z" in full else z // 2
+    zl = pl.ds(0, 2) if "z" in full else z % 2
+    x = pl.ds(0, 4) if "x" in full else pos["x"]
+    y = pl.ds(0, 4) if "y" in full else pos["y"]
+    return buf.at[zh, x, y, zl, pl.ds(rows[0], rows[1]), pl.ds(cols[0], cols[1])]
+
+
+def ring_gather(buf, send, recv):
+    me = place()
+    every = (0, 512)
+    halves = ((0, 256), (256, 256))
+    copies = []
+    for phase in range(3):
+        plans = []
+        for color in range(3):
+            axis = AXES[(color + phase) % 3]
+            full = [AXES[(color + p) % 3] for p in range(phase)]
+            plans.append((color, axis, full, COLOR_ROWS[color]))
+        first = {}
+        for color, axis, full, rows in plans:
+            here = region(buf, full, me, rows, every)
+            for side, by in ((0, 1), (1, -1)):
+                c = remote(
+                    here, here, send.at[color, phase, side], recv.at[color, phase, side],
+                    device_at(moved(me, axis, by)),
+                )
+                c.start()
+                first[color, side] = c
+        second = {}
+        for color, axis, full, rows in plans:
+            for side, by in ((0, 1), (1, -1)):
+                first[color, side].wait_recv()
+                came = region(buf, full, moved(me, axis, -by), rows, halves[side])
+                c = remote(
+                    came, came, send.at[color, phase, 2 + side], recv.at[color, phase, 2 + side],
+                    device_at(moved(me, axis, by)),
+                )
+                c.start()
+                second[color, side] = c
+        for key in second:
+            second[key].wait_recv()
+        copies += list(first.values()) + list(second.values())
+    for c in copies:
+        c.wait_send()
+
+
+def swap_small(buf, mine, peer, send, recv):
+    copies = []
+    for k in range(1, 8):
+        src, dst = mine(k)
+        c = remote(src, dst, send.at[k - 1], recv.at[k - 1], peer(k))
+        c.start()
+        copies.append(c)
+    for c in copies:
+        c.wait_recv()
+    return copies
+
+
+def merge_stats(buf):
+    tops = [buf[i, 0:1, :] for i in range(8)]
+    top = functools.reduce(jnp.maximum, tops)
+    total = sum(buf[i, 1:2, :] * jnp.exp(buf[i, 0:1, :] - top) for i in range(8))
+    target = sum(buf[i, 2:3, :] for i in range(8))
+    return top, total, target
+
+
+def head_body(
+    res_ref, gain_ref, head_ref, tgt_ref, out_ref,
+    buf, acc, sq, stats, join_e, join_t,
+    send, recv, sq_send, sq_recv, je_send, je_recv, jt_send, jt_recv,
+):
+    me = place()
+    e = lax.axis_index("expert")
+    t = lax.axis_index("tensor")
+    cross = 1 - 2 * (me["z"] % 2)
+    greet(
+        [tensor_peer(k) for k in range(1, 8)]
+        + [expert_peer(k) for k in range(1, 8)]
+        + [device_at(moved(me, "z", -cross))]
+    )
+    x = res_ref[...].astype(jnp.float32)
+    part = jnp.sum(x * x, axis=1, keepdims=True)
+    sq[t] = jnp.broadcast_to(part, (128, 128)).T[0:8]
+    small = swap_small(sq, lambda k: (sq.at[t], sq.at[t]), tensor_peer, sq_send, sq_recv)
+    squares = sum(sq[i] for i in range(8))[0:1]
+    scale = lax.rsqrt(squares / 4096.0 + epsilon)
+    column = jnp.broadcast_to(scale, (128, 128)).T
+    rows = (x * column[:, 0:1] * gain_ref[...]).astype(jnp.bfloat16)
+    buf[me["z"] // 2, me["x"], me["y"], me["z"] % 2] = rows
+    ring_gather(buf, send, recv)
+
+    acc[...] = jnp.zeros_like(acc)
+
+    @pl.loop(0, 8)
+    def _(k):
+        piece = buf[:, :, k // 2, k % 2].reshape(1024, 512)
+        acc[...] += jnp.dot(
+            piece, head_ref[pl.ds(k * 512, 512), :], preferred_element_type=jnp.float32
+        )
+
+    start = (e * 8 + t) * 500
+
+    @pl.loop(0, 8)
+    def _(i):
+        block = acc[pl.ds(i * 128, 128), :]
+        top = jnp.max(block, axis=1, keepdims=True)
+        total = jnp.sum(jnp.exp(block - top), axis=1, keepdims=True)
+        ids = lax.broadcasted_iota(jnp.int32, block.shape, 1) + start
+        hit = tgt_ref[pl.ds(i * 128, 128), :] == ids
+        target = jnp.sum(jnp.where(hit, block, 0.0), axis=1, keepdims=True)
+        lane = lax.broadcasted_iota(jnp.int32, (128, 128), 1)
+        three = jnp.where(lane == 0, top, jnp.where(lane == 1, total, target))
+        stats[i] = three.T[0:8]
+
+    join_e[e] = stats[e]
+    small += swap_small(
+        join_e, lambda k: (stats.at[(e + k) % 8], join_e.at[e]), expert_peer, je_send, je_recv
+    )
+    top, total, target = merge_stats(join_e)
+    join_t[t, 0:1] = top
+    join_t[t, 1:2] = total
+    join_t[t, 2:3] = target
+    join_t[t, 3:8] = jnp.zeros((5, 128), jnp.float32)
+    small += swap_small(
+        join_t, lambda k: (join_t.at[t], join_t.at[t]), tensor_peer, jt_send, jt_recv
+    )
+    top, total, target = merge_stats(join_t)
+    out_ref[...] = jnp.broadcast_to(top + jnp.log(total) - target, out_ref.shape)
+    for c in small:
+        c.wait_send()
+
+
+def head_loss(residual, gain, head_weight, targets):
+    vmem = pl.BlockSpec(memory_space=pltpu.VMEM)
+    sem = pltpu.SemaphoreType.DMA
+    return pl.pallas_call(
+        head_body,
+        out_shape=jax.ShapeDtypeStruct((8, 128), jnp.float32),
+        in_specs=[vmem] * 4,
+        out_specs=vmem,
+        scratch_shapes=[
+            pltpu.VMEM((2, 4, 4, 2, 128, 512), jnp.bfloat16),
+            pltpu.VMEM((1024, 500), jnp.float32),
+            pltpu.VMEM((8, 8, 128), jnp.float32),
+            pltpu.VMEM((8, 8, 128), jnp.float32),
+            pltpu.VMEM((8, 8, 128), jnp.float32),
+            pltpu.VMEM((8, 8, 128), jnp.float32),
+            sem((3, 3, 4)), sem((3, 3, 4)),
+            sem((7,)), sem((7,)), sem((7,)), sem((7,)), sem((7,)), sem((7,)),
+        ],
+        compiler_params=pltpu.CompilerParams(
+            collective_id=0, has_side_effects=True, vmem_limit_bytes=40 * 2**20
+        ),
+        name="head_loss",
+    )(residual, gain.reshape(1, 512), head_weight, targets.reshape(1024, 1))
 
 
 def on_device(
@@ -23,7 +220,6 @@
     experts = w_gate.shape[0] * n_expert
     capacity = 4 * tok_rows // experts
     slots_all = experts * capacity
-    vocab_part = head_weight.shape[1]
     token_float = tokens.astype(jnp.float32)
     first_squares = lax.psum(jnp.sum(token_float * token_float, axis=1), "tensor")
     normed = (
@@ -74,32 +270,9 @@
         precision=lax.Precision.HIGHEST,
     )
     residual = (token_float + mixed_rows).astype(jnp.bfloat16)
-    residual_float = residual.astype(jnp.float32)
-    second_squares = lax.psum(jnp.sum(residual_float * residual_float, axis=1), "tensor")
-    final_rows = (
-        residual_float
-        * lax.rsqrt(second_squares / full_width + epsilon)[:, None]
-        * final_gain[None, :]
-    ).astype(jnp.bfloat16)
-    final_pieces = lax.all_gather(final_rows[None], ("expert", "tensor"), axis=0, tiled=True)
-    all_rows = (
-        final_pieces.reshape(n_expert, n_tensor, tok_rows, slice_width)
-        .transpose(0, 2, 1, 3)
-        .reshape(n_expert * tok_rows, full_width)
-    )
-    logits = jnp.dot(all_rows, head_weight, preferred_element_type=jnp.float32)
-    vocab_start = (lax.axis_index("expert") * n_tensor + lax.axis_index("tensor")) * vocab_part
-    local_top = jnp.max(logits, axis=1)
-    local_total = jnp.sum(jnp.exp(logits - local_top[:, None]), axis=1)
-    target_hit = targets[:, None] - vocab_start == jnp.arange(vocab_part, dtype=jnp.int32)[None, :]
-    target_logit = jnp.sum(jnp.where(target_hit, logits, jnp.zeros_like(logits)), axis=1)
+    loss = head_loss(residual, final_gain, head_weight, targets)[0]
     own_rows = tok_rows // n_tensor
-    terms = jnp.stack([local_top, local_total, target_logit])
-    terms = merge_terms(lax.all_gather(terms, "expert"))
-    terms = lax.dynamic_slice_in_dim(terms, lax.axis_index("expert") * tok_rows, tok_rows, 1)
-    terms = merge_terms(lax.all_gather(terms, "tensor"))
-    loss_all = terms[0] + jnp.log(terms[1]) - terms[2]
-    return lax.dynamic_slice_in_dim(loss_all, lax.axis_index("tensor") * own_rows, own_rows)
+    return lax.dynamic_slice_in_dim(loss, lax.axis_index("tensor") * own_rows, own_rows)
 
 
 def solution(mesh):

time: 839 us -> 456 us (0.54)
  waiting for transfers between devices: 577 us -> 233 us
  blocking collectives: 115 us -> 37.9 us
  Pallas kernels: 0 us -> 70.6 us
  local copies, waits for them, and re-layouts: 71.5 us -> 56.5 us
  matrix products: 43.3 us -> 34.6 us
    all_gather x1 -> x0, waiting for transfers between devices: 337 us -> none  [on_device(): lax.all_gather(final_rows[None], ('expert', 'tensor'), axis=0, tiled=True)]
    pallas_call x0 -> x1, Pallas kernels: none -> 70.6 us  [head_loss(): pl.pallas_call(head_body, out_shape=jax.ShapeDtypeStruct((8, 128), jnp.fl...]
    all_gather x2 -> x0, blocking collectives: 57.9 us -> none  [the longest x1 34.2 us: on_device(): terms = merge_terms(lax.all_gather(terms, 'expert'))]
    psum x1 -> x0, blocking collectives: 18.8 us -> none  [on_device(): lax.psum(jnp.sum(residual_float * residual_float, axis=1), 'tensor')]
    reshape x1, local copies, waits for them, and re-layouts: 11.7 us -> 0.22 us  [head_loss(): targets.reshape(1024, 1)]
    dot_general x1 -> x0, matrix products: 8.43 us -> none  [on_device(): logits = jnp.dot(all_rows, head_weight, preferred_element_type=jnp.float32)]
    unnamed x22 -> x24, local copies, waits for them, and re-layouts: 37.6 us -> 34 us
  transfers between devices with their start and end apart: 4 -> 3, of which waited for: 4 -> 3; matrix products, arithmetic and copies ran while one was open for 0% -> 1% of each run, Pallas kernels for 0% -> 0%
where the time goes in v2:
time: 456 us; the launch traced here: 455 us
  waiting for transfers between devices  233 us (51%)
  Pallas kernels  70.6 us (15%)
  local copies, waits for them, and re-layouts  56.5 us (12%)
  blocking collectives  37.9 us (8%)
  matrix products  34.6 us (8%)
  between operations  13.6 us (3%)
  starting transfers between devices  6.32 us (1%)
    reduce_scatter x1, waiting for transfers between devices, on_device(): lax.psum_scatter(blocks, ('seq', 'tensor'), scatter_dimension=0, tiled=True)  181 us
    pallas_call x1, Pallas kernels, head_loss(): pl.pallas_call(head_body, out_shape=jax.ShapeDtypeStruct((8, 128), jnp.fl...  70.6 us
    all_gather x1, waiting for transfers between devices, on_device(): lax.all_gather(incoming[None], ('seq', 'tensor'), axis=0, tiled=True)  46.9 us
    unnamed x24, local copies, waits for them, and re-layouts  34 us
    psum x1, blocking collectives, on_device(): lax.psum(jnp.sum(token_float * token_float, axis=1), 'tensor')  20.4 us
    all_to_all x1, blocking collectives, on_device(): lax.all_to_all(outgoing, 'expert', split_axis=0, concat_axis=0, tiled=True)  17.4 us
    dot_general x1, matrix products, on_device(): up = jnp.dot(rows, w_up[0], preferred_element_type=jnp.float32)  12.7 us
    transpose x1, local copies, waits for them, and re-layouts, on_device(): rows = pieces.reshape(n_seq, n_tensor, slots_all, slice_width).transpose(...  11.4 us
  transfers between devices with their start and end apart: 3, of which 3 were waited for; matrix products, arithmetic and copies ran while one was open for 1% of the time, Pallas kernels for 0%

profile of v2, /device:TPU:0, one launch (start us, length us, event | category | flops | bytes accessed | tf_op | source)
XLA Modules:
  0.0 455.2 jit_solution(7131319594035589504)
XLA Ops:
  6.5 0.0 all-gather.3.cloned.1.call-start
  6.5 0.8 copy.35
  7.3 0.1 eq.85
  7.5 0.1 eq.81
  7.6 0.6 reduce-window.6
  8.2 0.2 slice_reduce_fusion
  8.5 0.1 fusion.27
  8.6 0.1 reshape.53
  8.7 0.1 copy.37
  8.8 0.7 multiply_add_fusion
  9.5 1.0 fusion.8
  10.5 20.4 %psum.7 = f32[128]{0:T(128)S(1)} all-reduce(f32[128]{0:T(128)S(1)} %fusion.8), channel_id=1, replica_groups=mesh['seq'=2,'expert'=8,'tensor'=8] {'tensor'}, use_global_device_ids=true, to_apply=%region_4.5 | all-reduce | flops 128 | bytes 1024 | tf_op jit(solution)/shard_map/psum | solution.py:224
  30.9 1.3 convolution_convert_fusion.1
  32.2 17.4 %all_to_all.10 = bf16[8,64,512]{2,1,0:T(8,128)(2,1)} all-to-all(bf16[8,64,512]{2,1,0:T(8,128)(2,1)S(1)} %bitcast.58), channel_id=1, replica_groups=mesh['seq'=2,'expert'=8,'tensor'=8] {'expert'}, dimensions={0} | all-to-all | bytes 1048576 | tf_op jit(solution)/shard_map/all_to_all | solution.py:242
  49.7 0.0 all-gather.3.cloned.1.call-update
  49.7 0.0 reduce-scatter.2.cloned.1.call-start
  49.7 46.9 %all-gather.3.cloned.1.call-done = bf16[128,64,512]{2,1,0:T(8,128)(2,1)} async-done(((bf16[8,64,512]{2,1,0:T(8,128)(2,1)}), bf16[128,64,512]{2,1,0:T(8,128)(2,1)}) %all-gather.3.cloned.1.call-update) | async-done | bytes 8388624 | tf_op jit(solution)/shard_map/all_gather | solution.py:243
  96.6 11.4 %copy.38 = bf16[2,512,8,512]{3,2,1,0:T(8,128)(2,1)} copy(bf16[2,512,8,512]{3,1,2,0:T(8,128)(2,1)} %bitcast.54) | data formatting | bytes 16777216 | tf_op jit(solution)/shard_map/transpose | solution.py:246
  108.0 0.0 slice-start
  108.0 12.3 %copy.42 = bf16[128,8,8,512]{3,1,2,0:T(8,128)(2,1)} copy(bf16[128,8,8,512]{3,2,1,0:T(8,128)(2,1)} %bitcast.52) | data formatting | bytes 16777216
  120.3 0.0 copy-start.2
  120.4 0.0 slice-start.1
  120.4 0.0 slice-start.2
  120.4 12.7 %fusion.1 = f32[1024,896]{1,0:T(8,128)S(1)} fusion(bf16[1024,4096]{1,0:T(8,128)(2,1)} %bitcast.55, bf16[1,4096,896]{2,1,0:T(8,128)(2,1)} %param.16), kind=kOutput, calls=%fused_computation.2 | convolution fusion | flops 7516192768 | bytes 19398656 | tf_op jit(solution)/shard_map/dot_general | solution.py:250
  133.0 0.0 slice-done
  133.0 0.0 copy-done.2
  133.0 0.0 slice-done.1
  133.1 0.0 slice-start.3
  133.1 9.2 %multiply_convert_fusion = bf16[1024,896]{1,0:T(8,128)(2,1)S(1)} fusion(f32[1024,896]{1,0:T(8,128)S(1)} %fusion.1, bf16[1024,4096]{1,0:T(8,128)(2,1)S(1)} %bitcast.56, bf16[1,4096,896]{2,1,0:T(8,128)(2,1)S(1)} %bitcast.63), kind=kOutput, calls=%fused_computation.6 | convolution fusion | flops 7521697792 | bytes 21233664 | tf_op jit(solution)/shard_map/dot_general | solution.py:249
  142.2 0.0 slice-done.2
  142.2 0.0 slice-done.3
  142.3 11.1 %convolution_convert_fusion = bf16[1024,4096]{1,0:T(8,128)(2,1)} fusion(bf16[1024,896]{1,0:T(8,128)(2,1)S(1)} %multiply_convert_fusion, bf16[1,896,4096]{2,1,0:T(8,128)(2,1)S(1)} %bitcast.65), kind=kOutput, calls=%fused_computation | convolution fusion | flops 7520387072 | bytes 17563648 | tf_op jit(solution)/shard_map/dot_general | solution.py:252
  153.3 12.2 %copy.43 = bf16[128,8,8,512]{3,2,1,0:T(8,128)(2,1)} copy(bf16[128,8,8,512]{3,1,2,0:T(8,128)(2,1)} %bitcast.57) | data formatting | bytes 16777216
  165.5 9.6 %copy.39 = bf16[2,512,8,512]{3,1,2,0:T(8,128)(2,1)} copy(bf16[2,512,8,512]{3,2,1,0:T(8,128)(2,1)} %bitcast.53) | data formatting | bytes 16777216 | tf_op jit(solution)/shard_map/reshape | solution.py:254
  175.1 0.0 copy-start.4
  175.1 0.0 copy-start.5
  175.1 0.0 copy-start.3
  175.1 0.0 reduce-scatter.2.cloned.1.call-update
  175.2 0.0 copy-start.1
  175.2 181.2 %reduce-scatter.2.cloned.1.call-done = bf16[512,512]{1,0:T(8,128)(2,1)} async-done(((bf16[8192,512]{1,0:T(8,128)(2,1)}), bf16[512,512]{1,0:T(8,128)(2,1)}) %reduce-scatter.2.cloned.1.call-update) | async-done | bytes 524304 | tf_op jit(solution)/shard_map/reduce_scatter | solution.py:258
  356.3 6.3 %all-to-all-start.1 = ((bf16[8,64,512]{2,1,0:T(8,128)(2,1)}), bf16[8,64,512]{2,1,0:T(8,128)(2,1)S(1)}, u32[]{:S(2)}, u32[]{:S(2)}) async-start(bf16[8,64,512]{2,1,0:T(8,128)(2,1)} %bitcast.59), calls=%async_computation.2 | async-start | bytes 1048576 | tf_op jit(solution)/shard_map/all_to_all | solution.py:260
  362.6 6.5 %copy.40.head_ref = bf16[4096,500]{1,0:T(8,128)(2,1)} copy(bf16[4096,500]{0,1:T(8,128)(2,1)} %param.18) | data formatting | bytes 8192000 | tf_op args[8]
  369.1 0.0 copy-done.4
  369.1 0.2 copy.41.tgt_ref
  369.3 0.0 copy-done.5
  369.4 5.1 %all-to-all-done.1 = bf16[8,64,512]{2,1,0:T(8,128)(2,1)S(1)} async-done(((bf16[8,64,512]{2,1,0:T(8,128)(2,1)}), bf16[8,64,512]{2,1,0:T(8,128)(2,1)S(1)}, u32[]{:S(2)}, u32[]{:S(2)}) %all-to-all-start.1) | async-done | bytes 524320 | tf_op jit(solution)/shard_map/all_to_all | solution.py:260
  374.5 0.0 copy-done.3
  374.5 0.5 fusion.7.res_ref
  374.9 0.0 copy-done.1
  375.0 0.0 copy-start
  375.0 2.2 copy-done
  377.1 70.6 %head_loss.1 = f32[8,128]{1,0:T(8,128)S(1)} custom-call(bf16[128,512]{1,0:T(8,128)(2,1)S(1)} %fusion.7.res_ref, f32[1,512]{1,0:T(1,128)S(1)} %bitcast.50, bf16[4096,500]{1,0:T(8,128)(2,1)S(1)} %copy-done, s32[1024,1]{1,0:T(8,128)S(1)} %copy.41.tgt_ref), custom_call_target="tpu_custom_call" | custom-call | tf_op jit(solution)/shard_map/head_loss/pallas_call | solution.py:190
  447.8 0.6 dynamic-slice_bitcast_fusion
  (9 shorter events, 0.1 us)
Async XLA Ops:
  6.5 90.1 %all-gather.3.cloned.1.call-start = ((), (), s32[]{:S(2)}) async-start(), calls=%async_computation.4 | async-start | bytes 8912896 | tf_op jit(solution)/shard_map/all_gather | solution.py:243
  49.7 306.7 %reduce-scatter.2.cloned.1.call-start = ((), (), s32[]{:S(2)}) async-start(), calls=%async_computation.3 | async-start | bytes 8912896 | tf_op jit(solution)/shard_map/reduce_scatter | solution.py:258
  108.0 25.0 %slice-start = ((s8[7340032]{0:T(1024)(128)(4,1)}), s8[3145728]{0:T(1024)(128)(4,1)S(1)}, s32[]{:S(2)}) async-start(s8[7340032]{0:T(1024)(128)(4,1)} %bitcast.62), calls=%async_computation.5 | async-start | bytes 6291456
  120.3 12.7 %copy-start.2 = (bf16[128,8,8,512]{3,1,2,0:T(8,128)(2,1)S(1)}, bf16[128,8,8,512]{3,1,2,0:T(8,128)(2,1)}, u32[]{:S(2)}) copy-start(bf16[128,8,8,512]{3,1,2,0:T(8,128)(2,1)} %copy.42) | copy-start | bytes 25165828
  120.4 12.7 %slice-start.1 = ((s8[7340032]{0:T(1024)(128)(4,1)}), s8[4194304]{0:T(1024)(128)(4,1)S(1)}, s32[]{:S(2)}) async-start(s8[7340032]{0:T(1024)(128)(4,1)} %bitcast.62), calls=%async_computation.6 | async-start | bytes 8388608
  120.4 21.9 %slice-start.2 = ((s8[7340032]{0:T(1024)(128)(4,1)}), s8[4194304]{0:T(1024)(128)(4,1)S(1)}, s32[]{:S(2)}) async-start(s8[7340032]{0:T(1024)(128)(4,1)} %bitcast.64), calls=%async_computation.7 | async-start | bytes 8388608
  133.1 9.2 %slice-start.3 = ((s8[7340032]{0:T(1024)(128)(4,1)}), s8[3145728]{0:T(1024)(128)(4,1)S(1)}, s32[]{:S(2)}) async-start(s8[7340032]{0:T(1024)(128)(4,1)} %bitcast.64), calls=%async_computation.8 | async-start | bytes 6291456
  175.1 194.0 %copy-start.4 = (s32[1024]{0:T(1024)S(1)}, s32[1024]{0:T(1024)}, u32[]{:S(2)}) copy-start(s32[1024]{0:T(1024)} %param.19) | copy-start | bytes 12292
  175.1 194.2 %copy-start.5 = (f32[128,2]{0,1:T(2,128)S(1)}, f32[128,2]{0,1:T(2,128)}, u32[]{:S(2)}) copy-start(f32[128,2]{0,1:T(2,128)} %param.12) | copy-start | bytes 3076
  175.1 199.4 %copy-start.3 = (bf16[128,512]{1,0:T(8,128)(2,1)S(1)}, bf16[128,512]{1,0:T(8,128)(2,1)}, u32[]{:S(2)}) copy-start(bf16[128,512]{1,0:T(8,128)(2,1)} %param.10) | copy-start | bytes 393220
  175.2 199.8 %copy-start.1 = (f32[512]{0:T(512)S(1)}, f32[512]{0:T(512)}, u32[]{:S(2)}) copy-start(f32[512]{0:T(512)} %param.14) | copy-start | bytes 6148
  356.3 18.2 %all-to-all-start.1 = ((bf16[8,64,512]{2,1,0:T(8,128)(2,1)}), bf16[8,64,512]{2,1,0:T(8,128)(2,1)S(1)}, u32[]{:S(2)}, u32[]{:S(2)}) async-start(bf16[8,64,512]{2,1,0:T(8,128)(2,1)} %bitcast.59), calls=%async_computation.2 | async-start | bytes 1048576 | tf_op jit(solution)/shard_map/all_to_all | solution.py:260
  375.0 2.2 copy-start
Sparse Core Ops, SparseCore 0:
  49.8 46.7 all-gather.2
  175.3 181.0 reduce-scatter.1

commit v3 on v2

--- a/solution.py
+++ b/solution.py
@@ -209,69 +209,348 @@
     )(residual, gain.reshape(1, 512), head_weight, targets.reshape(1024, 1))
 
 
+CHUNKS = 2
+CHUNK_ROWS = 256
+Z_FIRST = (0, 144)
+Y_FIRST = (144, 112)
+HIDDEN_TILES = ((0, 256), (256, 256), (512, 256), (768, 128))
+
+
+class Lane:
+    def __init__(self, send, recv, chunk):
+        self.send, self.recv, self.chunk, self.used, self.copies = send, recv, chunk, 0, []
+
+    def start(self, src, dst, dev):
+        c = remote(
+            src, dst, self.send.at[self.chunk, self.used], self.recv.at[self.chunk, self.used], dev
+        )
+        self.used += 1
+        c.start()
+        self.copies.append(c)
+        return c
+
+    def finish(self):
+        for c in self.copies:
+            c.wait_send()
+
+
+def expert_body(
+    tok_ref, gain_ref, routes_ref, weights_ref, wg_hbm, wu_hbm, wd_hbm, out_ref,
+    wg, wu, wd, sent, X, hidden, part, twin, ra1, ra2, ra3, rb1, rb2, rb3, back, sq,
+    w_sem, sq_send, sq_recv, g_send, g_recv, r_send, r_recv,
+):
+    me = place()
+    s = lax.axis_index("seq")
+    e = lax.axis_index("expert")
+    t = lax.axis_index("tensor")
+    y, zl = me["y"], t % 2
+    f32, bf16 = jnp.float32, jnp.bfloat16
+    loads = [
+        pltpu.make_async_copy(src.at[0], dst, w_sem.at[i])
+        for i, (src, dst) in enumerate(((wg_hbm, wg), (wu_hbm, wu), (wd_hbm, wd)))
+    ]
+    for c in loads:
+        c.start()
+    twin_dev = (1 - s, e, t)
+    pair_dev = (s, e, y * 2 + 1 - zl)
+
+    def y_dev(by):
+        return (s, e, ((y + by + 4) % 4) * 2 + zl)
+
+    def at_y(by):
+        return (y + by + 4) % 4
+
+    greet(
+        [tensor_peer(k) for k in range(1, 8)]
+        + [expert_peer(k) for k in range(1, 8)]
+        + [twin_dev]
+    )
+    x = tok_ref[...].astype(f32)
+    sq[t] = jnp.broadcast_to(jnp.sum(x * x, axis=1, keepdims=True), (128, 128)).T[0:8]
+    small = swap_small(sq, lambda k: (sq.at[t], sq.at[t]), tensor_peer, sq_send, sq_recv)
+    squares = sum(sq[i] for i in range(8))[0:1]
+    column = jnp.broadcast_to(lax.rsqrt(squares / 4096.0 + epsilon), (128, 128)).T
+    normed = (x * column[:, 0:1] * gain_ref[...]).astype(bf16)
+    names = [routes_ref[j : j + 1, :] for j in range(2)]
+    ids = lax.broadcasted_iota(jnp.int32, (8, 128), 0)
+    named = ((names[0] == ids) | (names[1] == ids)).astype(f32)
+    lower = (
+        lax.broadcasted_iota(jnp.int32, (128, 128), 0)
+        < lax.broadcasted_iota(jnp.int32, (128, 128), 1)
+    ).astype(f32)
+    earlier = jnp.dot(named, lower, preferred_element_type=f32)
+    slot_ids = lax.broadcasted_iota(jnp.int32, (32, 128), 0).astype(f32)
+
+    def selection(j, chunk, i):
+        own = earlier[i : i + 1] == slot_ids + 32.0 * chunk
+        if j is None:
+            hit = named[i : i + 1] > 0.5
+        else:
+            hit = names[j] == i
+        return jnp.where(own & hit, 1.0, 0.0)
+
+    for chunk in range(CHUNKS):
+        pick = jnp.concatenate([selection(None, chunk, i) for i in range(8)], axis=0)
+        sent[chunk] = jnp.dot(
+            pick.astype(bf16), normed, preferred_element_type=f32
+        ).astype(bf16)
+
+    def cols(first, n):
+        return pl.ds(pl.multiple_of(first, 256), n)
+
+    def rows_of(i):
+        return pl.ds(pl.multiple_of(i * 32, 32), 32)
+
+    lanes = [Lane(g_send, g_recv, c) for c in range(CHUNKS)]
+    sums = [Lane(r_send, r_recv, c) for c in range(CHUNKS)]
+    own_cols = cols(t * 512, 512)
+    arrivals = []
+    for chunk in range(CHUNKS):
+        X[chunk, s, rows_of(e), own_cols] = sent[chunk, rows_of(e), :]
+        arrivals.append([
+            lanes[chunk].start(
+                sent.at[chunk, rows_of((e + k) % 8)],
+                X.at[chunk, s, rows_of(e), own_cols],
+                expert_peer(k),
+            )
+            for k in range(1, 8)
+        ])
+
+    def gather(chunk):
+        lane = lanes[chunk]
+
+        def view(rows, first, n):
+            return X.at[chunk, s, pl.ds(*rows), cols(first, n)]
+
+        def put(rows, first, n, dev):
+            v = view(rows, first, n)
+            return lane.start(v, v, dev)
+
+        for c in arrivals[chunk]:
+            c.wait_recv()
+        az = put(Z_FIRST, t * 512, 512, pair_dev)
+        by = [put(Y_FIRST, t * 512, 512, y_dev(d)) for d in (1, -1)]
+        bz = [put(Y_FIRST, t * 512, 512, pair_dev)]
+        yield
+        az.wait_recv()
+        ay = [put(Z_FIRST, y * 1024, 1024, y_dev(d)) for d in (1, -1)]
+        twins = [put(Z_FIRST, y * 1024, 1024, twin_dev)]
+        bh = []
+        for side, d in ((0, 1), (1, -1)):
+            by[side].wait_recv()
+            first = (at_y(-d) * 2 + zl) * 512
+            bh.append(put(Y_FIRST, first + 256 * side, 256, y_dev(d)))
+            bz.append(put(Y_FIRST, first, 512, pair_dev))
+        yield
+        ah = []
+        for side, d in ((0, 1), (1, -1)):
+            ay[side].wait_recv()
+            first = at_y(-d) * 1024
+            ah.append(put(Z_FIRST, first + 512 * side, 512, y_dev(d)))
+            twins.append(put(Z_FIRST, first, 1024, twin_dev))
+        for c in bh:
+            c.wait_recv()
+        bz.append(put(Y_FIRST, (at_y(2) * 2 + zl) * 512, 512, pair_dev))
+        for i, d in enumerate((0, -1, 1)):
+            bz[i].wait_recv()
+            twins.append(put(Y_FIRST, at_y(d) * 1024, 1024, twin_dev))
+        yield
+        for c in ah:
+            c.wait_recv()
+        twins.append(put(Z_FIRST, at_y(2) * 1024, 1024, twin_dev))
+        bz[3].wait_recv()
+        twins.append(put(Y_FIRST, at_y(2) * 1024, 1024, twin_dev))
+        yield
+        for c in twins:
+            c.wait_recv()
+
+    pending = [[] for _ in range(CHUNKS)]
+
+    def compute(chunk):
+        def up_step(first, n):
+            def step():
+                rows = X[chunk].reshape(2 * CHUNK_ROWS, 4096)
+                gate = jnp.dot(rows, wg[:, first : first + n], preferred_element_type=f32)
+                up = jnp.dot(rows, wu[:, first : first + n], preferred_element_type=f32)
+                hidden[:, first : first + n] = (gate / (1.0 + jnp.exp(-gate)) * up).astype(bf16)
+            return step
+
+        def down_step(k):
+            def step():
+                first = k * 512
+                done = jnp.dot(hidden[...], wd[:, first : first + 512], preferred_element_type=f32)
+                part[chunk, :, :, first : first + 512] = done.astype(bf16).reshape(
+                    2, CHUNK_ROWS, 512
+                )
+                pending[chunk].append(
+                    sums[chunk].start(
+                        part.at[chunk, 1 - s, :, pl.ds(first, 512)],
+                        twin.at[chunk, :, pl.ds(first, 512)],
+                        twin_dev,
+                    )
+                )
+            return step
+
+        return [up_step(*tile) for tile in HIDDEN_TILES] + [down_step(k) for k in range(8)]
+
+    def reduce(chunk):
+        lane = sums[chunk]
+
+        def add(rows, first, n, *others):
+            block = part[chunk, s, pl.ds(*rows), cols(first, n)].astype(f32)
+            for o in others:
+                block = block + o.astype(f32)
+            part[chunk, s, pl.ds(*rows), cols(first, n)] = block.astype(bf16)
+
+        def put(rows, first, n, dst, dev):
+            return lane.start(part.at[chunk, s, pl.ds(*rows), cols(first, n)], dst, dev)
+
+        for k in range(8):
+            pending[chunk][k].wait_recv()
+            first = k * 512
+            part[chunk, s, :, first : first + 512] = (
+                part[chunk, s, :, first : first + 512].astype(f32)
+                + twin[chunk, :, first : first + 512].astype(f32)
+            ).astype(bf16)
+        a1 = [
+            put(Z_FIRST, at_y(2) * 1024 + 512 * h, 512, ra1.at[chunk, h], y_dev(d))
+            for h, d in ((0, -1), (1, 1))
+        ]
+        b1 = [
+            put(Y_FIRST, (at_y(d) * 2 + 1 - zl) * 512, 512, rb1.at[chunk, i], pair_dev)
+            for i, d in enumerate((2, 1, -1, 0))
+        ]
+        yield
+        b1[0].wait_recv()
+        add(Y_FIRST, (at_y(2) * 2 + zl) * 512, 512, rb1[chunk, 0])
+        b2 = [
+            put(Y_FIRST, (at_y(2) * 2 + zl) * 512 + 256 * h, 256, rb2.at[chunk, h], y_dev(d))
+            for h, d in ((0, -1), (1, 1))
+        ]
+        a2 = []
+        for h, d in ((0, -1), (1, 1)):
+            a1[h].wait_recv()
+            add(Z_FIRST, at_y(d) * 1024 + 512 * h, 512, ra1[chunk, h])
+            a2.append(put(Z_FIRST, at_y(d) * 1024, 1024, ra2.at[chunk, h], y_dev(d)))
+        yield
+        for i, d in ((1, 1), (2, -1), (3, 0)):
+            b1[i].wait_recv()
+            add(Y_FIRST, (at_y(d) * 2 + zl) * 512, 512, rb1[chunk, i])
+        b3 = []
+        for h, d in ((0, -1), (1, 1)):
+            b2[h].wait_recv()
+            first = (at_y(d) * 2 + zl) * 512
+            add(Y_FIRST, first + 256 * h, 256, rb2[chunk, h])
+            b3.append(put(Y_FIRST, first, 512, rb3.at[chunk, h], y_dev(d)))
+        yield
+        for c in a2:
+            c.wait_recv()
+        add(Z_FIRST, y * 1024, 1024, ra2[chunk, 0], ra2[chunk, 1])
+        a3 = put(Z_FIRST, (y * 2 + 1 - zl) * 512, 512, ra3.at[chunk], pair_dev)
+        for c in b3:
+            c.wait_recv()
+        add(Y_FIRST, t * 512, 512, rb3[chunk, 0], rb3[chunk, 1])
+        yield
+        a3.wait_recv()
+        add(Z_FIRST, t * 512, 512, ra3[chunk])
+        back[chunk, rows_of(e), :] = part[chunk, s, rows_of(e), own_cols]
+        homes = [
+            lane.start(
+                part.at[chunk, s, rows_of((e + k) % 8), own_cols],
+                back.at[chunk, rows_of(e)],
+                expert_peer(k),
+            )
+            for k in range(1, 8)
+        ]
+        yield
+        for c in homes:
+            c.wait_recv()
+
+    def drain(moves):
+        for _ in moves:
+            pass
+
+    def weave(steps, moves, every):
+        for i, step in enumerate(steps):
+            step()
+            if (i + 1) % every == 0:
+                next(moves, None)
+        drain(moves)
+
+    first_moves, later_moves = gather(0), gather(1)
+    for _ in range(4):
+        next(first_moves, None)
+    next(later_moves, None)
+    drain(first_moves)
+    for c in loads:
+        c.wait()
+    weave(compute(0), later_moves, 1)
+    back_moves = reduce(0)
+    next(back_moves, None)
+    weave(compute(1), back_moves, 1)
+    drain(reduce(1))
+
+    mixed = jnp.zeros((128, 512), f32)
+    for j in range(2):
+        total = jnp.zeros((128, 512), f32)
+        for chunk in range(CHUNKS):
+            pick = jnp.concatenate([selection(j, chunk, i) for i in range(8)], axis=0)
+            total = total + lax.dot_general(
+                pick.T.astype(bf16), back[chunk], (((1,), (0,)), ((), ())),
+                preferred_element_type=f32,
+            )
+        mixed = mixed + weights_ref[:, j : j + 1] * total
+    out_ref[...] = (x + mixed).astype(bf16)
+    for c in small:
+        c.wait_send()
+    for lane in lanes + sums:
+        lane.finish()
+
+
+def expert_layer(tokens, gain, routes, route_weights, w_gate, w_up, w_down):
+    vmem = pl.BlockSpec(memory_space=pltpu.VMEM)
+    hbm = pl.BlockSpec(memory_space=pl.ANY)
+    sem = pltpu.SemaphoreType.DMA
+    bf16 = jnp.bfloat16
+    a, b = Z_FIRST[1], Y_FIRST[1]
+    return pl.pallas_call(
+        expert_body,
+        out_shape=jax.ShapeDtypeStruct((128, 512), bf16),
+        in_specs=[vmem] * 4 + [hbm] * 3,
+        out_specs=vmem,
+        scratch_shapes=[
+            pltpu.VMEM((4096, 896), bf16),
+            pltpu.VMEM((4096, 896), bf16),
+            pltpu.VMEM((896, 4096), bf16),
+            pltpu.VMEM((CHUNKS, CHUNK_ROWS, 512), bf16),
+            pltpu.VMEM((CHUNKS, 2, CHUNK_ROWS, 4096), bf16),
+            pltpu.VMEM((2 * CHUNK_ROWS, 896), bf16),
+            pltpu.VMEM((CHUNKS, 2, CHUNK_ROWS, 4096), bf16),
+            pltpu.VMEM((CHUNKS, CHUNK_ROWS, 4096), bf16),
+            pltpu.VMEM((CHUNKS, 2, a, 512), bf16),
+            pltpu.VMEM((CHUNKS, 2, a, 1024), bf16),
+            pltpu.VMEM((CHUNKS, a, 512), bf16),
+            pltpu.VMEM((CHUNKS, 4, b, 512), bf16),
+            pltpu.VMEM((CHUNKS, 2, b, 256), bf16),
+            pltpu.VMEM((CHUNKS, 2, b, 512), bf16),
+            pltpu.VMEM((CHUNKS, CHUNK_ROWS, 512), bf16),
+            pltpu.VMEM((8, 8, 128), jnp.float32),
+            sem((3,)), sem((7,)), sem((7,)),
+            sem((CHUNKS, 32)), sem((CHUNKS, 32)), sem((CHUNKS, 32)), sem((CHUNKS, 32)),
+        ],
+        compiler_params=pltpu.CompilerParams(
+            collective_id=1, has_side_effects=True, vmem_limit_bytes=62 * 2**20
+        ),
+        name="expert_layer",
+    )(tokens, gain.reshape(1, 512), routes.T, route_weights, w_gate, w_up, w_down)
+
+
 def on_device(
     tokens, routes, route_weights, norm_gain, final_gain, w_gate, w_up, w_down, head_weight, targets
 ):
-    tok_rows, slice_width = tokens.shape
-    n_seq = lax.axis_size("seq")
-    n_expert = lax.axis_size("expert")
-    n_tensor = lax.axis_size("tensor")
-    full_width = slice_width * n_tensor
-    experts = w_gate.shape[0] * n_expert
-    capacity = 4 * tok_rows // experts
-    slots_all = experts * capacity
-    token_float = tokens.astype(jnp.float32)
-    first_squares = lax.psum(jnp.sum(token_float * token_float, axis=1), "tensor")
-    normed = (
-        token_float * lax.rsqrt(first_squares / full_width + epsilon)[:, None] * norm_gain[None, :]
-    ).astype(jnp.bfloat16)
-    expert_ids = jnp.arange(experts, dtype=jnp.int32)
-    onehot = (routes.reshape(-1)[:, None] == expert_ids[None, :]).astype(jnp.int32)
-    earlier = jnp.cumsum(onehot, axis=0) - onehot
-    slot_index = jnp.sum(earlier * onehot, axis=1).reshape(tok_rows, 2)
-    place_index = routes * capacity + slot_index
-    positions = jnp.arange(slots_all, dtype=jnp.int32)
-    first_hit = place_index[None, :, 0] == positions[:, None]
-    second_hit = place_index[None, :, 1] == positions[:, None]
-    dispatch = (first_hit | second_hit).astype(jnp.bfloat16)
-    outgoing = (
-        jnp.dot(dispatch, normed, preferred_element_type=jnp.float32)
-        .astype(jnp.bfloat16)
-        .reshape(experts, capacity, slice_width)
-    )
-    incoming = lax.all_to_all(outgoing, "expert", split_axis=0, concat_axis=0, tiled=True)
-    pieces = lax.all_gather(incoming[None], ("seq", "tensor"), axis=0, tiled=True)
-    rows = (
-        pieces.reshape(n_seq, n_tensor, slots_all, slice_width)
-        .transpose(0, 2, 1, 3)
-        .reshape(n_seq * slots_all, full_width)
-    )
-    gate = jnp.dot(rows, w_gate[0], preferred_element_type=jnp.float32)
-    up = jnp.dot(rows, w_up[0], preferred_element_type=jnp.float32)
-    hidden = (jax.nn.silu(gate) * up).astype(jnp.bfloat16)
-    partial = jnp.dot(hidden, w_down[0], preferred_element_type=jnp.float32).astype(jnp.bfloat16)
-    blocks = (
-        partial.reshape(n_seq, slots_all, n_tensor, slice_width)
-        .transpose(0, 2, 1, 3)
-        .reshape(n_seq * n_tensor * slots_all, slice_width)
-    )
-    expert_out = lax.psum_scatter(blocks, ("seq", "tensor"), scatter_dimension=0, tiled=True)
-    outgoing_back = expert_out.astype(jnp.bfloat16).reshape(experts, capacity, slice_width)
-    returned = lax.all_to_all(outgoing_back, "expert", split_axis=0, concat_axis=0, tiled=True)
-    combine_matrix = route_weights[:, 0:1] * (place_index[:, 0:1] == positions[None, :]).astype(
-        jnp.float32
-    )
-    combine_matrix = combine_matrix + route_weights[:, 1:2] * (
-        place_index[:, 1:2] == positions[None, :]
-    ).astype(jnp.float32)
-    mixed_rows = jnp.dot(
-        combine_matrix,
-        returned.reshape(slots_all, slice_width).astype(jnp.float32),
-        precision=lax.Precision.HIGHEST,
-    )
-    residual = (token_float + mixed_rows).astype(jnp.bfloat16)
+    residual = expert_layer(tokens, norm_gain, routes, route_weights, w_gate, w_up, w_down)
     loss = head_loss(residual, final_gain, head_weight, targets)[0]
-    own_rows = tok_rows // n_tensor
+    own_rows = tokens.shape[0] // 8
     return lax.dynamic_slice_in_dim(loss, lax.axis_index("tensor") * own_rows, own_rows)
 
 

time: 456 us -> 208 us (0.46)
  waiting for transfers between devices: 233 us -> 0 us
  Pallas kernels: 70.6 us -> 197 us
  local copies, waits for them, and re-layouts: 56.5 us -> 10.9 us
  blocking collectives: 37.9 us -> 0 us
  matrix products: 34.6 us -> 0 us
  between operations: 13.6 us -> 0.09 us
  starting transfers between devices: 6.32 us -> 0 us
    reduce_scatter x1 -> x0, waiting for transfers between devices: 181 us -> none  [on_device(): lax.psum_scatter(blocks, ('seq', 'tensor'), scatter_dimension=0, tiled=True)]
    pallas_call x0 -> x1, Pallas kernels: none -> 128 us  [expert_layer(): pl.pallas_call(expert_body, out_shape=jax.ShapeDtypeStruct((128, 512), bf...]
    all_gather x1 -> x0, waiting for transfers between devices: 46.9 us -> none  [on_device(): lax.all_gather(incoming[None], ('seq', 'tensor'), axis=0, tiled=True)]
    dot_general x5 -> x0, matrix products: 34.6 us -> none  [the longest x1 12.7 us: on_device(): up = jnp.dot(rows, w_up[0], preferred_element_type=jnp.float32)]
    unnamed x24 -> x10, local copies, waits for them, and re-layouts: 34 us -> 10.1 us
    psum x1 -> x0, blocking collectives: 20.4 us -> none  [on_device(): lax.psum(jnp.sum(token_float * token_float, axis=1), 'tensor')]
    all_to_all x1 -> x0, blocking collectives: 17.4 us -> none  [on_device(): lax.all_to_all(outgoing, 'expert', split_axis=0, concat_axis=0, tiled=True)]
    transpose x1 -> x0, local copies, waits for them, and re-layouts: 11.4 us -> none  [on_device(): rows = pieces.reshape(n_seq, n_tensor, slots_all, slice_width).transpose(...]
  transfers between devices with their start and end apart: 3 -> 0, of which waited for: 3 -> 0; matrix products, arithmetic and copies ran while one was open for 1% -> 0% of each run, Pallas kernels for 0% -> 0%
where the time goes in v3:
time: 208 us
  Pallas kernels  197 us (95%)
  local copies, waits for them, and re-layouts  10.9 us (5%)
    pallas_call x1, Pallas kernels, expert_layer(): pl.pallas_call(expert_body, out_shape=jax.ShapeDtypeStruct((128, 512), bf...  128 us
    pallas_call x1, Pallas kernels, head_loss(): pl.pallas_call(head_body, out_shape=jax.ShapeDtypeStruct((8, 128), jnp.fl...  69.4 us
    unnamed x10, local copies, waits for them, and re-layouts  10.1 us

profile of v3, /device:TPU:0, one launch (start us, length us, event | category | flops | bytes accessed | tf_op | source)
XLA Modules:
  0.0 208.2 jit_solution(8230970345744413591)
XLA Ops:
  0.0 1.4 copy.13.weights_ref
  1.4 127.7 %expert_layer.1.res_ref = bf16[128,512]{1,0:T(8,128)(2,1)} custom-call(bf16[128,512]{1,0:T(8,128)(2,1)} %tok_ref.1, f32[1,512]{1,0:T(1,128)} %bitcast.8, s32[2,128]{1,0:T(2,128)} %bitcast.9, f32[128,2]{1,0:T(8,128)} %copy.13.weights_ref, bf16[1,4096,896]{2,1,0:T(8,128)(2,1)} %wg_hbm.1, bf16[1,4096,896]{2,1,0:T(8,128)(2,1)} %wu_hbm.1, ...), custom_call_target="tpu_custom_call" | custom-call | tf_op jit(solution)/shard_map/expert_layer/pallas_call | solution.py:516
  129.1 0.0 copy-start.3
  129.1 0.0 copy-start.1
  129.1 0.0 copy-start.2
  129.1 6.5 %copy.14.head_ref = bf16[4096,500]{1,0:T(8,128)(2,1)} copy(bf16[4096,500]{0,1:T(8,128)(2,1)} %param.18) | data formatting | bytes 8192000 | tf_op args[8]
  135.7 0.0 copy-done.3
  135.7 0.2 copy.15.tgt_ref
  135.9 0.0 copy-done.1
  135.9 0.0 copy-done.2
  135.9 0.0 copy-start
  135.9 2.2 %copy-done = bf16[4096,500]{1,0:T(8,128)(2,1)S(1)} copy-done((bf16[4096,500]{1,0:T(8,128)(2,1)S(1)}, bf16[4096,500]{1,0:T(8,128)(2,1)}, u32[]{:S(2)}) %copy-start) | copy-done | bytes 4096024
  138.1 69.4 %head_loss.1 = f32[8,128]{1,0:T(8,128)S(1)} custom-call(bf16[128,512]{1,0:T(8,128)(2,1)S(1)} %copy-done.1, f32[1,512]{1,0:T(1,128)S(1)} %bitcast.6, bf16[4096,500]{1,0:T(8,128)(2,1)S(1)} %copy-done, s32[1024,1]{1,0:T(8,128)S(1)} %copy.15.tgt_ref), custom_call_target="tpu_custom_call" | custom-call | tf_op jit(solution)/shard_map/head_loss/pallas_call | solution.py:190
  207.6 0.6 dynamic-slice_bitcast_fusion
  (1 shorter events, 0.0 us)
Async XLA Ops:
  129.1 6.6 %copy-start.3 = (s32[1024]{0:T(1024)S(1)}, s32[1024]{0:T(1024)}, u32[]{:S(2)}) copy-start(s32[1024]{0:T(1024)} %param.19) | copy-start | bytes 12292
  129.1 6.8 %copy-start.1 = (bf16[128,512]{1,0:T(8,128)(2,1)S(1)}, bf16[128,512]{1,0:T(8,128)(2,1)}, u32[]{:S(2)}) copy-start(bf16[128,512]{1,0:T(8,128)(2,1)} %expert_layer.1.res_ref) | copy-start | bytes 393220
  129.1 6.8 %copy-start.2 = (f32[512]{0:T(512)S(1)}, f32[512]{0:T(512)}, u32[]{:S(2)}) copy-start(f32[512]{0:T(512)} %param.14) | copy-start | bytes 6148
  135.9 2.2 %copy-start = (bf16[4096,500]{1,0:T(8,128)(2,1)S(1)}, bf16[4096,500]{1,0:T(8,128)(2,1)}, u32[]{:S(2)}) copy-start(bf16[4096,500]{1,0:T(8,128)(2,1)} %copy.14.head_ref) | copy-start | bytes 12288004

commit v4 on v3

--- a/solution.py
+++ b/solution.py
@@ -47,7 +47,6 @@
     barrier = pltpu.get_barrier_semaphore()
     for dev in peers:
         pl.semaphore_signal(barrier, inc=1, device_id=dev, device_id_type=MESH)
-    pl.semaphore_wait(barrier, len(peers))
 
 
 def region(buf, full, pos, rows, cols):
@@ -94,6 +93,7 @@
         for key in second:
             second[key].wait_recv()
         copies += list(first.values()) + list(second.values())
+        yield
     for c in copies:
         c.wait_send()
 
@@ -105,9 +105,17 @@
         c = remote(src, dst, send.at[k - 1], recv.at[k - 1], peer(k))
         c.start()
         copies.append(c)
+    return copies
+
+
+def arrived(copies):
     for c in copies:
         c.wait_recv()
     return copies
+
+
+def squares_row(x):
+    return jnp.broadcast_to(jnp.sum(x * x, axis=1, keepdims=True), (128, 128)).T[0:8]
 
 
 def merge_stats(buf):
@@ -118,101 +126,78 @@
     return top, total, target
 
 
-def head_body(
-    res_ref, gain_ref, head_ref, tgt_ref, out_ref,
-    buf, acc, sq, stats, join_e, join_t,
-    send, recv, sq_send, sq_recv, je_send, je_recv, jt_send, jt_recv,
+def head_part(
+    x, gain_ref, head_load, head_t, tgt_ref, out_ref, buf, acc, sq, stats, join_e, join_t,
+    send, recv, sq_send, sq_recv, je_send, je_recv, jt_send, jt_recv, scales, sc_send, sc_recv,
 ):
     me = place()
     e = lax.axis_index("expert")
     t = lax.axis_index("tensor")
-    cross = 1 - 2 * (me["z"] % 2)
-    greet(
-        [tensor_peer(k) for k in range(1, 8)]
-        + [expert_peer(k) for k in range(1, 8)]
-        + [device_at(moved(me, "z", -cross))]
+    sq[t] = squares_row(x)
+    buf[me["z"] // 2, me["x"], me["y"], me["z"] % 2] = (x * gain_ref[...]).astype(jnp.bfloat16)
+    moves = ring_gather(buf, send, recv)
+    small = swap_small(sq, lambda k: (sq.at[t], sq.at[t]), tensor_peer, sq_send, sq_recv)
+    next(moves)
+    arrived(small)
+    scales[e] = lax.rsqrt(sum(sq[i] for i in range(8)) / 4096.0 + epsilon)
+    spread = swap_small(
+        scales, lambda k: (scales.at[e], scales.at[e]), expert_peer, sc_send, sc_recv
     )
-    x = res_ref[...].astype(jnp.float32)
-    part = jnp.sum(x * x, axis=1, keepdims=True)
-    sq[t] = jnp.broadcast_to(part, (128, 128)).T[0:8]
-    small = swap_small(sq, lambda k: (sq.at[t], sq.at[t]), tensor_peer, sq_send, sq_recv)
-    squares = sum(sq[i] for i in range(8))[0:1]
-    scale = lax.rsqrt(squares / 4096.0 + epsilon)
-    column = jnp.broadcast_to(scale, (128, 128)).T
-    rows = (x * column[:, 0:1] * gain_ref[...]).astype(jnp.bfloat16)
-    buf[me["z"] // 2, me["x"], me["y"], me["z"] % 2] = rows
-    ring_gather(buf, send, recv)
-
+    next(moves)
+    next(moves)
+    next(moves, None)
+    small += arrived(spread)
+
+    head_load.wait()
     acc[...] = jnp.zeros_like(acc)
 
     @pl.loop(0, 8)
     def _(k):
         piece = buf[:, :, k // 2, k % 2].reshape(1024, 512)
-        acc[...] += jnp.dot(
-            piece, head_ref[pl.ds(k * 512, 512), :], preferred_element_type=jnp.float32
+        acc[...] += lax.dot_general(
+            piece, head_t[:, pl.ds(pl.multiple_of(k * 512, 512), 512)], (((1,), (1,)), ((), ())),
+            preferred_element_type=jnp.float32,
         )
 
     start = (e * 8 + t) * 500
 
     @pl.loop(0, 8)
     def _(i):
-        block = acc[pl.ds(i * 128, 128), :]
+        column = jnp.broadcast_to(scales[i, 0:1, :], (128, 128)).T
+        block = acc[pl.ds(i * 128, 128), :] * column[:, 0:1]
         top = jnp.max(block, axis=1, keepdims=True)
         total = jnp.sum(jnp.exp(block - top), axis=1, keepdims=True)
-        ids = lax.broadcasted_iota(jnp.int32, block.shape, 1) + start
-        hit = tgt_ref[pl.ds(i * 128, 128), :] == ids
+        ids = (lax.broadcasted_iota(jnp.int32, block.shape, 1) + start).astype(jnp.float32)
+        wanted = jnp.broadcast_to(tgt_ref[i].astype(jnp.float32), (128, 128)).T
+        hit = wanted[:, 0:1] == ids
         target = jnp.sum(jnp.where(hit, block, 0.0), axis=1, keepdims=True)
         lane = lax.broadcasted_iota(jnp.int32, (128, 128), 1)
         three = jnp.where(lane == 0, top, jnp.where(lane == 1, total, target))
         stats[i] = three.T[0:8]
 
     join_e[e] = stats[e]
-    small += swap_small(
+    small += arrived(swap_small(
         join_e, lambda k: (stats.at[(e + k) % 8], join_e.at[e]), expert_peer, je_send, je_recv
-    )
+    ))
     top, total, target = merge_stats(join_e)
     join_t[t, 0:1] = top
     join_t[t, 1:2] = total
     join_t[t, 2:3] = target
     join_t[t, 3:8] = jnp.zeros((5, 128), jnp.float32)
-    small += swap_small(
+    small += arrived(swap_small(
         join_t, lambda k: (join_t.at[t], join_t.at[t]), tensor_peer, jt_send, jt_recv
-    )
+    ))
     top, total, target = merge_stats(join_t)
     out_ref[...] = jnp.broadcast_to(top + jnp.log(total) - target, out_ref.shape)
     for c in small:
         c.wait_send()
 
 
-def head_loss(residual, gain, head_weight, targets):
-    vmem = pl.BlockSpec(memory_space=pltpu.VMEM)
-    sem = pltpu.SemaphoreType.DMA
-    return pl.pallas_call(
-        head_body,
-        out_shape=jax.ShapeDtypeStruct((8, 128), jnp.float32),
-        in_specs=[vmem] * 4,
-        out_specs=vmem,
-        scratch_shapes=[
-            pltpu.VMEM((2, 4, 4, 2, 128, 512), jnp.bfloat16),
-            pltpu.VMEM((1024, 500), jnp.float32),
-            pltpu.VMEM((8, 8, 128), jnp.float32),
-            pltpu.VMEM((8, 8, 128), jnp.float32),
-            pltpu.VMEM((8, 8, 128), jnp.float32),
-            pltpu.VMEM((8, 8, 128), jnp.float32),
-            sem((3, 3, 4)), sem((3, 3, 4)),
-            sem((7,)), sem((7,)), sem((7,)), sem((7,)), sem((7,)), sem((7,)),
-        ],
-        compiler_params=pltpu.CompilerParams(
-            collective_id=0, has_side_effects=True, vmem_limit_bytes=40 * 2**20
-        ),
-        name="head_loss",
-    )(residual, gain.reshape(1, 512), head_weight, targets.reshape(1024, 1))
-
-
-CHUNKS = 2
-CHUNK_ROWS = 256
-Z_FIRST = (0, 144)
-Y_FIRST = (144, 112)
+CHUNKS = 4
+SLOTS = 16
+CHUNK_ROWS = 8 * SLOTS
+Z_FIRST = (0, 80)
+Y_FIRST = (80, 48)
 HIDDEN_TILES = ((0, 256), (256, 256), (512, 256), (768, 128))
 
 
@@ -235,9 +220,13 @@
 
 
 def expert_body(
-    tok_ref, gain_ref, routes_ref, weights_ref, wg_hbm, wu_hbm, wd_hbm, out_ref,
-    wg, wu, wd, sent, X, hidden, part, twin, ra1, ra2, ra3, rb1, rb2, rb3, back, sq,
+    tok_ref, gain_ref, routes_ref, weights_ref, final_ref, tgt_ref,
+    wg_hbm, wu_hbm, wd_hbm, head_hbm, out_ref,
+    wg, wu, wd, head_t, sent, X, hidden, part, twin, ra1, ra2, ra3, rb1, rb2, rb3, back, sq,
+    buf, acc, sq2, stats, join_e, join_t,
     w_sem, sq_send, sq_recv, g_send, g_recv, r_send, r_recv,
+    h_send, h_recv, s2_send, s2_recv, je_send, je_recv, jt_send, jt_recv,
+    scales, sc_send, sc_recv, slot_out, slot_in, so_send, so_recv, tw_send, tw_recv,
 ):
     me = place()
     s = lax.axis_index("seq")
@@ -249,8 +238,10 @@
         pltpu.make_async_copy(src.at[0], dst, w_sem.at[i])
         for i, (src, dst) in enumerate(((wg_hbm, wg), (wu_hbm, wu), (wd_hbm, wd)))
     ]
+    head_load = pltpu.make_async_copy(head_hbm, head_t, w_sem.at[3])
     for c in loads:
         c.start()
+    head_load.start()
     twin_dev = (1 - s, e, t)
     pair_dev = (s, e, y * 2 + 1 - zl)
 
@@ -263,14 +254,11 @@
     greet(
         [tensor_peer(k) for k in range(1, 8)]
         + [expert_peer(k) for k in range(1, 8)]
-        + [twin_dev]
+        + [twin_dev, device_at(moved(me, "z", 2 * zl - 1))]
     )
     x = tok_ref[...].astype(f32)
-    sq[t] = jnp.broadcast_to(jnp.sum(x * x, axis=1, keepdims=True), (128, 128)).T[0:8]
-    small = swap_small(sq, lambda k: (sq.at[t], sq.at[t]), tensor_peer, sq_send, sq_recv)
-    squares = sum(sq[i] for i in range(8))[0:1]
-    column = jnp.broadcast_to(lax.rsqrt(squares / 4096.0 + epsilon), (128, 128)).T
-    normed = (x * column[:, 0:1] * gain_ref[...]).astype(bf16)
+    sq[t] = squares_row(x)
+    weighted = (x * gain_ref[...]).astype(bf16)
     names = [routes_ref[j : j + 1, :] for j in range(2)]
     ids = lax.broadcasted_iota(jnp.int32, (8, 128), 0)
     named = ((names[0] == ids) | (names[1] == ids)).astype(f32)
@@ -279,10 +267,10 @@
         < lax.broadcasted_iota(jnp.int32, (128, 128), 1)
     ).astype(f32)
     earlier = jnp.dot(named, lower, preferred_element_type=f32)
-    slot_ids = lax.broadcasted_iota(jnp.int32, (32, 128), 0).astype(f32)
+    slot_ids = lax.broadcasted_iota(jnp.int32, (SLOTS, 128), 0).astype(f32)
 
     def selection(j, chunk, i):
-        own = earlier[i : i + 1] == slot_ids + 32.0 * chunk
+        own = earlier[i : i + 1] == slot_ids + float(SLOTS * chunk)
         if j is None:
             hit = named[i : i + 1] > 0.5
         else:
@@ -292,14 +280,16 @@
     for chunk in range(CHUNKS):
         pick = jnp.concatenate([selection(None, chunk, i) for i in range(8)], axis=0)
         sent[chunk] = jnp.dot(
-            pick.astype(bf16), normed, preferred_element_type=f32
+            pick.astype(bf16), weighted, preferred_element_type=f32
         ).astype(bf16)
+    pl.semaphore_wait(pltpu.get_barrier_semaphore(), 16)
+    small = swap_small(sq, lambda k: (sq.at[t], sq.at[t]), tensor_peer, sq_send, sq_recv)
 
     def cols(first, n):
         return pl.ds(pl.multiple_of(first, 256), n)
 
     def rows_of(i):
-        return pl.ds(pl.multiple_of(i * 32, 32), 32)
+        return pl.ds(pl.multiple_of(i * SLOTS, SLOTS), SLOTS)
 
     lanes = [Lane(g_send, g_recv, c) for c in range(CHUNKS)]
     sums = [Lane(r_send, r_recv, c) for c in range(CHUNKS)]
@@ -370,8 +360,9 @@
         def up_step(first, n):
             def step():
                 rows = X[chunk].reshape(2 * CHUNK_ROWS, 4096)
-                gate = jnp.dot(rows, wg[:, first : first + n], preferred_element_type=f32)
-                up = jnp.dot(rows, wu[:, first : first + n], preferred_element_type=f32)
+                scale = slot_in[:, :, chunk].reshape(2 * CHUNK_ROWS, 128)[:, 0:1]
+                gate = jnp.dot(rows, wg[:, first : first + n], preferred_element_type=f32) * scale
+                up = jnp.dot(rows, wu[:, first : first + n], preferred_element_type=f32) * scale
                 hidden[:, first : first + n] = (gate / (1.0 + jnp.exp(-gate)) * up).astype(bf16)
             return step
 
@@ -466,29 +457,48 @@
         for c in homes:
             c.wait_recv()
 
-    def drain(moves):
-        for _ in moves:
-            pass
-
-    def weave(steps, moves, every):
+    g = [gather(c) for c in range(CHUNKS)]
+    r = [reduce(c) for c in range(CHUNKS)]
+
+    def weave(steps, moves):
+        done = 0
         for i, step in enumerate(steps):
             step()
-            if (i + 1) % every == 0:
-                next(moves, None)
-        drain(moves)
-
-    first_moves, later_moves = gather(0), gather(1)
-    for _ in range(4):
-        next(first_moves, None)
-    next(later_moves, None)
-    drain(first_moves)
+            upto = (i + 1) * len(moves) // len(steps)
+            for m in moves[done:upto]:
+                next(m, None)
+            done = upto
+
+    def advance(order, moves):
+        for c in order:
+            next(moves[c], None)
+
+    advance((0, 1), g)
+    arrived(small)
+    factor = lax.rsqrt(sum(sq[i] for i in range(8))[0:1] / 4096.0 + epsilon)
+    for i in range(8):
+        for chunk in range(CHUNKS):
+            picked = jnp.sum(selection(None, chunk, i) * factor, axis=1, keepdims=True)
+            slot_out[i, chunk] = jnp.broadcast_to(picked, (SLOTS, 128))
+    slot_in[s, e] = slot_out[e]
+    factors = swap_small(
+        slot_in, lambda k: (slot_out.at[(e + k) % 8], slot_in.at[s, e]), expert_peer,
+        so_send, so_recv,
+    )
+    advance((0, 2, 1, 0, 3, 2), g)
+    arrived(factors)
+    crossing = remote(slot_in.at[s], slot_in.at[s], tw_send.at[0], tw_recv.at[0], twin_dev)
+    crossing.start()
+    advance((1, 0, 3, 2, 0), g)
+    crossing.wait_recv()
+    small += factors + [crossing]
     for c in loads:
         c.wait()
-    weave(compute(0), later_moves, 1)
-    back_moves = reduce(0)
-    next(back_moves, None)
-    weave(compute(1), back_moves, 1)
-    drain(reduce(1))
+    weave(compute(0), [g[1], g[3], g[2], g[1]])
+    weave(compute(1), [r[0], g[3], g[2], r[0], g[3]])
+    weave(compute(2), [r[0], r[1], r[0], r[1]])
+    weave(compute(3), [r[0], r[1], r[2], r[0], r[1], r[2]])
+    advance((3, 1, 2, 3, 1, 2, 3, 2, 3, 2, 3, 3), r)
 
     mixed = jnp.zeros((128, 512), f32)
     for j in range(2):
@@ -500,28 +510,36 @@
                 preferred_element_type=f32,
             )
         mixed = mixed + weights_ref[:, j : j + 1] * total
-    out_ref[...] = (x + mixed).astype(bf16)
+    residual = (x + mixed).astype(bf16).astype(f32)
+    head_part(
+        residual, final_ref, head_load, head_t, tgt_ref, out_ref, buf, acc, sq2, stats, join_e, join_t,
+        h_send, h_recv, s2_send, s2_recv, je_send, je_recv, jt_send, jt_recv,
+        scales, sc_send, sc_recv,
+    )
     for c in small:
         c.wait_send()
     for lane in lanes + sums:
         lane.finish()
 
 
-def expert_layer(tokens, gain, routes, route_weights, w_gate, w_up, w_down):
+def layer_loss(
+    tokens, gain, routes, route_weights, final_gain, targets, w_gate, w_up, w_down, head_weight
+):
     vmem = pl.BlockSpec(memory_space=pltpu.VMEM)
     hbm = pl.BlockSpec(memory_space=pl.ANY)
     sem = pltpu.SemaphoreType.DMA
-    bf16 = jnp.bfloat16
+    bf16, f32 = jnp.bfloat16, jnp.float32
     a, b = Z_FIRST[1], Y_FIRST[1]
     return pl.pallas_call(
         expert_body,
-        out_shape=jax.ShapeDtypeStruct((128, 512), bf16),
-        in_specs=[vmem] * 4 + [hbm] * 3,
+        out_shape=jax.ShapeDtypeStruct((8, 128), f32),
+        in_specs=[vmem] * 6 + [hbm] * 4,
         out_specs=vmem,
         scratch_shapes=[
             pltpu.VMEM((4096, 896), bf16),
             pltpu.VMEM((4096, 896), bf16),
             pltpu.VMEM((896, 4096), bf16),
+            pltpu.VMEM((500, 4096), bf16),
             pltpu.VMEM((CHUNKS, CHUNK_ROWS, 512), bf16),
             pltpu.VMEM((CHUNKS, 2, CHUNK_ROWS, 4096), bf16),
             pltpu.VMEM((2 * CHUNK_ROWS, 896), bf16),
@@ -534,22 +552,39 @@
             pltpu.VMEM((CHUNKS, 2, b, 256), bf16),
             pltpu.VMEM((CHUNKS, 2, b, 512), bf16),
             pltpu.VMEM((CHUNKS, CHUNK_ROWS, 512), bf16),
-            pltpu.VMEM((8, 8, 128), jnp.float32),
-            sem((3,)), sem((7,)), sem((7,)),
+            pltpu.VMEM((8, 8, 128), f32),
+            pltpu.VMEM((2, 4, 4, 2, 128, 512), bf16),
+            pltpu.VMEM((1024, 500), f32),
+            pltpu.VMEM((8, 8, 128), f32),
+            pltpu.VMEM((8, 8, 128), f32),
+            pltpu.VMEM((8, 8, 128), f32),
+            pltpu.VMEM((8, 8, 128), f32),
+            sem((4,)), sem((7,)), sem((7,)),
             sem((CHUNKS, 32)), sem((CHUNKS, 32)), sem((CHUNKS, 32)), sem((CHUNKS, 32)),
+            sem((3, 3, 4)), sem((3, 3, 4)),
+            sem((7,)), sem((7,)), sem((7,)), sem((7,)), sem((7,)), sem((7,)),
+            pltpu.VMEM((8, 8, 128), f32), sem((7,)), sem((7,)),
+            pltpu.VMEM((8, CHUNKS, SLOTS, 128), f32),
+            pltpu.VMEM((2, 8, CHUNKS, SLOTS, 128), f32),
+            sem((7,)), sem((7,)), sem((1,)), sem((1,)),
         ],
         compiler_params=pltpu.CompilerParams(
-            collective_id=1, has_side_effects=True, vmem_limit_bytes=62 * 2**20
+            collective_id=0, has_side_effects=True, vmem_limit_bytes=67043328
         ),
-        name="expert_layer",
-    )(tokens, gain.reshape(1, 512), routes.T, route_weights, w_gate, w_up, w_down)
+        name="layer_loss",
+    )(
+        tokens, gain.reshape(1, 512), routes.T, route_weights, final_gain.reshape(1, 512),
+        targets.reshape(8, 1, 128), w_gate, w_up, w_down, head_weight.T,
+    )
 
 
 def on_device(
     tokens, routes, route_weights, norm_gain, final_gain, w_gate, w_up, w_down, head_weight, targets
 ):
-    residual = expert_layer(tokens, norm_gain, routes, route_weights, w_gate, w_up, w_down)
-    loss = head_loss(residual, final_gain, head_weight, targets)[0]
+    loss = layer_loss(
+        tokens, norm_gain, routes, route_weights, final_gain, targets, w_gate, w_up, w_down,
+        head_weight,
+    )[0]
     own_rows = tokens.shape[0] // 8
     return lax.dynamic_slice_in_dim(loss, lax.axis_index("tensor") * own_rows, own_rows)
 

time: 208 us -> 174 us (0.84)
  Pallas kernels: 197 us -> 171 us
  local copies, waits for them, and re-layouts: 10.9 us -> 2.66 us
    pallas_call x2 -> x1, Pallas kernels: 197 us -> 171 us  [layer_loss(): pl.pallas_call(expert_body, out_shape=jax.ShapeDtypeStruct((8, 128), f32)...]
    unnamed x10 -> x1, local copies, waits for them, and re-layouts: 10.1 us -> 1.4 us
where the time goes in v4:
time: 174 us
  Pallas kernels  171 us (98%)
  local copies, waits for them, and re-layouts  2.66 us (2%)
    pallas_call x1, Pallas kernels, layer_loss(): pl.pallas_call(expert_body, out_shape=jax.ShapeDtypeStruct((8, 128), f32)...  171 us

profile of v4, /device:TPU:0, one launch (start us, length us, event | category | flops | bytes accessed | tf_op | source)
XLA Modules:
  0.0 174.0 jit_solution(3433951238781888590)
XLA Ops:
  0.0 1.4 copy.11.weights_ref
  1.4 171.3 %layer_loss.1 = f32[8,128]{1,0:T(8,128)} custom-call(bf16[128,512]{1,0:T(8,128)(2,1)} %tok_ref.1, f32[1,512]{1,0:T(1,128)} %bitcast.9, s32[2,128]{1,0:T(2,128)} %bitcast.11, f32[128,2]{1,0:T(8,128)} %copy.11.weights_ref, f32[1,512]{1,0:T(1,128)} %bitcast.10, s32[8,1,128]{2,1,0:T(1,128)} %bitcast.8, bf16[1,4096,896]{2,1,0:T(8,128)(2,1)} %wg_hbm.1, ...), custom_call_target="tpu_custom_call" | custom-call | tf_op jit(solution)/shard_map/layer_loss/pallas_call | solution.py:533
  172.8 0.7 slice.3
  173.4 0.6 dynamic-slice_bitcast_fusion

commit v5 on v4

--- a/solution.py
+++ b/solution.py
@@ -8,7 +8,16 @@
 
 epsilon = 1e-05
 MESH = pl.DeviceIdType.MESH
-COLOR_ROWS = ((0, 48), (48, 48), (96, 32))
+PIECES = (
+    ((0, 32, 0, 512), (32, 16, 0, 384)),
+    ((48, 32, 0, 512), (80, 16, 0, 384)),
+    ((96, 32, 0, 512), (32, 16, 384, 128), (80, 16, 384, 128)),
+)
+PASSED = (
+    (((0, 32, 0, 256), 0), ((32, 16, 0, 128), 1)), (((0, 32, 256, 256), 0), ((32, 16, 128, 256), 1)),
+    (((48, 32, 0, 256), 0), ((80, 16, 0, 256), 1)), (((48, 32, 256, 256), 0), ((80, 16, 256, 128), 1)),
+    (((96, 32, 0, 256), 0), ((32, 16, 384, 128), 1)), (((96, 32, 256, 256), 0), ((80, 16, 384, 128), 2)),
+)
 AXES = "xyz"
 
 
@@ -49,50 +58,58 @@
         pl.semaphore_signal(barrier, inc=1, device_id=dev, device_id_type=MESH)
 
 
-def region(buf, full, pos, rows, cols):
+def region(buf, full, pos, piece):
+    row, rows, col, cols = piece
     z = pos["z"]
     zh = pl.ds(0, 2) if "z" in full else z // 2
     zl = pl.ds(0, 2) if "z" in full else z % 2
     x = pl.ds(0, 4) if "x" in full else pos["x"]
     y = pl.ds(0, 4) if "y" in full else pos["y"]
-    return buf.at[zh, x, y, zl, pl.ds(rows[0], rows[1]), pl.ds(cols[0], cols[1])]
+    return buf.at[zh, x, y, zl, pl.ds(row, rows), pl.ds(col, cols)]
 
 
 def ring_gather(buf, send, recv):
     me = place()
-    every = (0, 512)
-    halves = ((0, 256), (256, 256))
     copies = []
     for phase in range(3):
-        plans = []
-        for color in range(3):
-            axis = AXES[(color + phase) % 3]
-            full = [AXES[(color + p) % 3] for p in range(phase)]
-            plans.append((color, axis, full, COLOR_ROWS[color]))
         first = {}
-        for color, axis, full, rows in plans:
-            here = region(buf, full, me, rows, every)
-            for side, by in ((0, 1), (1, -1)):
-                c = remote(
-                    here, here, send.at[color, phase, side], recv.at[color, phase, side],
-                    device_at(moved(me, axis, by)),
-                )
-                c.start()
-                first[color, side] = c
-        second = {}
-        for color, axis, full, rows in plans:
-            for side, by in ((0, 1), (1, -1)):
-                first[color, side].wait_recv()
-                came = region(buf, full, moved(me, axis, -by), rows, halves[side])
-                c = remote(
-                    came, came, send.at[color, phase, 2 + side], recv.at[color, phase, 2 + side],
-                    device_at(moved(me, axis, by)),
-                )
-                c.start()
-                second[color, side] = c
-        for key in second:
-            second[key].wait_recv()
-        copies += list(first.values()) + list(second.values())
+        used = [0, 0, 0]
+
+        def put(color, pos, full, piece, axis, by):
+            ref = region(buf, full, pos, piece)
+            k = used[color]
+            used[color] += 1
+            c = remote(
+                ref, ref, send.at[color, phase, k], recv.at[color, phase, k],
+                device_at(moved(me, axis, by)),
+            )
+            c.start()
+            copies.append(c)
+            return c
+
+        lines = [
+            (color, AXES[(color + phase) % 3], [AXES[(color + p) % 3] for p in range(phase)])
+            for color in range(3)
+        ]
+        for color, axis, full in lines:
+            for i, piece in enumerate(PIECES[color]):
+                for side, by in ((0, 1), (1, -1)):
+                    first[color, side, i] = put(color, me, full, piece, axis, by)
+        second = []
+        waited = set()
+        for turn in range(2):
+            for color, axis, full in lines:
+                for side, by in ((0, 1), (1, -1)):
+                    piece, source = PASSED[2 * color + side][turn]
+                    if (color, side, source) not in waited:
+                        waited.add((color, side, source))
+                        first[color, side, source].wait_recv()
+                    second.append(put(color, moved(me, axis, -by), full, piece, axis, by))
+        for key in first:
+            if key not in waited:
+                first[key].wait_recv()
+        for c in second:
+            c.wait_recv()
         yield
     for c in copies:
         c.wait_send()
@@ -127,7 +144,7 @@
 
 
 def head_part(
-    x, gain_ref, head_load, head_t, tgt_ref, out_ref, buf, acc, sq, stats, join_e, join_t,
+    x, gain_ref, head_load, head_t, tgt_ref, out_ref, buf, sq, stats, join_e, join_t,
     send, recv, sq_send, sq_recv, je_send, je_recv, jt_send, jt_recv, scales, sc_send, sc_recv,
 ):
     me = place()
@@ -149,31 +166,32 @@
     small += arrived(spread)
 
     head_load.wait()
-    acc[...] = jnp.zeros_like(acc)
-
-    @pl.loop(0, 8)
-    def _(k):
-        piece = buf[:, :, k // 2, k % 2].reshape(1024, 512)
-        acc[...] += lax.dot_general(
-            piece, head_t[:, pl.ds(pl.multiple_of(k * 512, 512), 512)], (((1,), (1,)), ((), ())),
-            preferred_element_type=jnp.float32,
-        )
-
     start = (e * 8 + t) * 500
 
-    @pl.loop(0, 8)
-    def _(i):
+    def block_terms(i, block):
         column = jnp.broadcast_to(scales[i, 0:1, :], (128, 128)).T
-        block = acc[pl.ds(i * 128, 128), :] * column[:, 0:1]
+        block = block * column[:, 0:1]
         top = jnp.max(block, axis=1, keepdims=True)
         total = jnp.sum(jnp.exp(block - top), axis=1, keepdims=True)
         ids = (lax.broadcasted_iota(jnp.int32, block.shape, 1) + start).astype(jnp.float32)
         wanted = jnp.broadcast_to(tgt_ref[i].astype(jnp.float32), (128, 128)).T
-        hit = wanted[:, 0:1] == ids
-        target = jnp.sum(jnp.where(hit, block, 0.0), axis=1, keepdims=True)
+        target = jnp.sum(jnp.where(wanted[:, 0:1] == ids, block, 0.0), axis=1, keepdims=True)
         lane = lax.broadcasted_iota(jnp.int32, (128, 128), 1)
         three = jnp.where(lane == 0, top, jnp.where(lane == 1, total, target))
         stats[i] = three.T[0:8]
+
+    @pl.loop(0, 2)
+    def _(zh):
+        for pair in range(2):
+            logits = jnp.zeros((256, 500), jnp.float32)
+            for k in range(8):
+                piece = buf[zh, 2 * pair : 2 * pair + 2, k // 2, k % 2].reshape(256, 512)
+                logits = logits + lax.dot_general(
+                    piece, head_t[:, k * 512 : k * 512 + 512], (((1,), (1,)), ((), ())),
+                    preferred_element_type=jnp.float32,
+                )
+            for j in range(2):
+                block_terms(zh * 4 + 2 * pair + j, logits[128 * j : 128 * j + 128])
 
     join_e[e] = stats[e]
     small += arrived(swap_small(
@@ -196,8 +214,7 @@
 CHUNKS = 4
 SLOTS = 16
 CHUNK_ROWS = 8 * SLOTS
-Z_FIRST = (0, 80)
-Y_FIRST = (80, 48)
+SPLITS = (80, 64, 80, 64)
 HIDDEN_TILES = ((0, 256), (256, 256), (512, 256), (768, 128))
 
 
@@ -219,11 +236,16 @@
             c.wait_send()
 
 
+def parts_of(chunk):
+    n = SPLITS[chunk]
+    return (0, n), (n, CHUNK_ROWS - n)
+
+
 def expert_body(
     tok_ref, gain_ref, routes_ref, weights_ref, final_ref, tgt_ref,
     wg_hbm, wu_hbm, wd_hbm, head_hbm, out_ref,
     wg, wu, wd, head_t, sent, X, hidden, part, twin, ra1, ra2, ra3, rb1, rb2, rb3, back, sq,
-    buf, acc, sq2, stats, join_e, join_t,
+    buf, sq2, stats, join_e, join_t,
     w_sem, sq_send, sq_recv, g_send, g_recv, r_send, r_recv,
     h_send, h_recv, s2_send, s2_recv, je_send, je_recv, jt_send, jt_recv,
     scales, sc_send, sc_recv, slot_out, slot_in, so_send, so_recv, tw_send, tw_recv,
@@ -308,6 +330,7 @@
 
     def gather(chunk):
         lane = lanes[chunk]
+        z_rows, y_rows = parts_of(chunk)
 
         def view(rows, first, n):
             return X.at[chunk, s, pl.ds(*rows), cols(first, n)]
@@ -318,38 +341,38 @@
 
         for c in arrivals[chunk]:
             c.wait_recv()
-        az = put(Z_FIRST, t * 512, 512, pair_dev)
-        by = [put(Y_FIRST, t * 512, 512, y_dev(d)) for d in (1, -1)]
-        bz = [put(Y_FIRST, t * 512, 512, pair_dev)]
+        az = put(z_rows, t * 512, 512, pair_dev)
+        by = [put(y_rows, t * 512, 512, y_dev(d)) for d in (1, -1)]
+        bz = [put(y_rows, t * 512, 512, pair_dev)]
         yield
         az.wait_recv()
-        ay = [put(Z_FIRST, y * 1024, 1024, y_dev(d)) for d in (1, -1)]
-        twins = [put(Z_FIRST, y * 1024, 1024, twin_dev)]
+        ay = [put(z_rows, y * 1024, 1024, y_dev(d)) for d in (1, -1)]
+        twins = [put(z_rows, y * 1024, 1024, twin_dev)]
         bh = []
         for side, d in ((0, 1), (1, -1)):
             by[side].wait_recv()
             first = (at_y(-d) * 2 + zl) * 512
-            bh.append(put(Y_FIRST, first + 256 * side, 256, y_dev(d)))
-            bz.append(put(Y_FIRST, first, 512, pair_dev))
+            bh.append(put(y_rows, first + 256 * side, 256, y_dev(d)))
+            bz.append(put(y_rows, first, 512, pair_dev))
         yield
         ah = []
         for side, d in ((0, 1), (1, -1)):
             ay[side].wait_recv()
             first = at_y(-d) * 1024
-            ah.append(put(Z_FIRST, first + 512 * side, 512, y_dev(d)))
-            twins.append(put(Z_FIRST, first, 1024, twin_dev))
+            ah.append(put(z_rows, first + 512 * side, 512, y_dev(d)))
+            twins.append(put(z_rows, first, 1024, twin_dev))
         for c in bh:
             c.wait_recv()
-        bz.append(put(Y_FIRST, (at_y(2) * 2 + zl) * 512, 512, pair_dev))
+        bz.append(put(y_rows, (at_y(2) * 2 + zl) * 512, 512, pair_dev))
         for i, d in enumerate((0, -1, 1)):
             bz[i].wait_recv()
-            twins.append(put(Y_FIRST, at_y(d) * 1024, 1024, twin_dev))
+            twins.append(put(y_rows, at_y(d) * 1024, 1024, twin_dev))
         yield
         for c in ah:
             c.wait_recv()
-        twins.append(put(Z_FIRST, at_y(2) * 1024, 1024, twin_dev))
+        twins.append(put(z_rows, at_y(2) * 1024, 1024, twin_dev))
         bz[3].wait_recv()
-        twins.append(put(Y_FIRST, at_y(2) * 1024, 1024, twin_dev))
+        twins.append(put(y_rows, at_y(2) * 1024, 1024, twin_dev))
         yield
         for c in twins:
             c.wait_recv()
@@ -386,6 +409,7 @@
 
     def reduce(chunk):
         lane = sums[chunk]
+        z_rows, y_rows = parts_of(chunk)
 
         def add(rows, first, n, *others):
             block = part[chunk, s, pl.ds(*rows), cols(first, n)].astype(f32)
@@ -404,46 +428,46 @@
                 + twin[chunk, :, first : first + 512].astype(f32)
             ).astype(bf16)
         a1 = [
-            put(Z_FIRST, at_y(2) * 1024 + 512 * h, 512, ra1.at[chunk, h], y_dev(d))
+            put(z_rows, at_y(2) * 1024 + 512 * h, 512, ra1.at[chunk, h, pl.ds(0, z_rows[1])], y_dev(d))
             for h, d in ((0, -1), (1, 1))
         ]
         b1 = [
-            put(Y_FIRST, (at_y(d) * 2 + 1 - zl) * 512, 512, rb1.at[chunk, i], pair_dev)
+            put(y_rows, (at_y(d) * 2 + 1 - zl) * 512, 512, rb1.at[chunk, i, pl.ds(0, y_rows[1])], pair_dev)
             for i, d in enumerate((2, 1, -1, 0))
         ]
         yield
         b1[0].wait_recv()
-        add(Y_FIRST, (at_y(2) * 2 + zl) * 512, 512, rb1[chunk, 0])
+        add(y_rows, (at_y(2) * 2 + zl) * 512, 512, rb1[chunk, 0, : y_rows[1]])
         b2 = [
-            put(Y_FIRST, (at_y(2) * 2 + zl) * 512 + 256 * h, 256, rb2.at[chunk, h], y_dev(d))
+            put(y_rows, (at_y(2) * 2 + zl) * 512 + 256 * h, 256, rb2.at[chunk, h, pl.ds(0, y_rows[1])], y_dev(d))
             for h, d in ((0, -1), (1, 1))
         ]
         a2 = []
         for h, d in ((0, -1), (1, 1)):
             a1[h].wait_recv()
-            add(Z_FIRST, at_y(d) * 1024 + 512 * h, 512, ra1[chunk, h])
-            a2.append(put(Z_FIRST, at_y(d) * 1024, 1024, ra2.at[chunk, h], y_dev(d)))
+            add(z_rows, at_y(d) * 1024 + 512 * h, 512, ra1[chunk, h, : z_rows[1]])
+            a2.append(put(z_rows, at_y(d) * 1024, 1024, ra2.at[chunk, h, pl.ds(0, z_rows[1])], y_dev(d)))
         yield
         for i, d in ((1, 1), (2, -1), (3, 0)):
             b1[i].wait_recv()
-            add(Y_FIRST, (at_y(d) * 2 + zl) * 512, 512, rb1[chunk, i])
+            add(y_rows, (at_y(d) * 2 + zl) * 512, 512, rb1[chunk, i, : y_rows[1]])
         b3 = []
         for h, d in ((0, -1), (1, 1)):
             b2[h].wait_recv()
             first = (at_y(d) * 2 + zl) * 512
-            add(Y_FIRST, first + 256 * h, 256, rb2[chunk, h])
-            b3.append(put(Y_FIRST, first, 512, rb3.at[chunk, h], y_dev(d)))
+            add(y_rows, first + 256 * h, 256, rb2[chunk, h, : y_rows[1]])
+            b3.append(put(y_rows, first, 512, rb3.at[chunk, h, pl.ds(0, y_rows[1])], y_dev(d)))
         yield
         for c in a2:
             c.wait_recv()
-        add(Z_FIRST, y * 1024, 1024, ra2[chunk, 0], ra2[chunk, 1])
-        a3 = put(Z_FIRST, (y * 2 + 1 - zl) * 512, 512, ra3.at[chunk], pair_dev)
+        add(z_rows, y * 1024, 1024, ra2[chunk, 0, : z_rows[1]], ra2[chunk, 1, : z_rows[1]])
+        a3 = put(z_rows, (y * 2 + 1 - zl) * 512, 512, ra3.at[chunk, pl.ds(0, z_rows[1])], pair_dev)
         for c in b3:
             c.wait_recv()
-        add(Y_FIRST, t * 512, 512, rb3[chunk, 0], rb3[chunk, 1])
+        add(y_rows, t * 512, 512, rb3[chunk, 0, : y_rows[1]], rb3[chunk, 1, : y_rows[1]])
         yield
         a3.wait_recv()
-        add(Z_FIRST, t * 512, 512, ra3[chunk])
+        add(z_rows, t * 512, 512, ra3[chunk, : z_rows[1]])
         back[chunk, rows_of(e), :] = part[chunk, s, rows_of(e), own_cols]
         homes = [
             lane.start(
@@ -512,7 +536,7 @@
         mixed = mixed + weights_ref[:, j : j + 1] * total
     residual = (x + mixed).astype(bf16).astype(f32)
     head_part(
-        residual, final_ref, head_load, head_t, tgt_ref, out_ref, buf, acc, sq2, stats, join_e, join_t,
+        residual, final_ref, head_load, head_t, tgt_ref, out_ref, buf, sq2, stats, join_e, join_t,
         h_send, h_recv, s2_send, s2_recv, je_send, je_recv, jt_send, jt_recv,
         scales, sc_send, sc_recv,
     )
@@ -529,7 +553,7 @@
     hbm = pl.BlockSpec(memory_space=pl.ANY)
     sem = pltpu.SemaphoreType.DMA
     bf16, f32 = jnp.bfloat16, jnp.float32
-    a, b = Z_FIRST[1], Y_FIRST[1]
+    a, b = max(SPLITS), CHUNK_ROWS - min(SPLITS)
     return pl.pallas_call(
         expert_body,
         out_shape=jax.ShapeDtypeStruct((8, 128), f32),
@@ -554,14 +578,13 @@
             pltpu.VMEM((CHUNKS, CHUNK_ROWS, 512), bf16),
             pltpu.VMEM((8, 8, 128), f32),
             pltpu.VMEM((2, 4, 4, 2, 128, 512), bf16),
-            pltpu.VMEM((1024, 500), f32),
             pltpu.VMEM((8, 8, 128), f32),
             pltpu.VMEM((8, 8, 128), f32),
             pltpu.VMEM((8, 8, 128), f32),
             pltpu.VMEM((8, 8, 128), f32),
             sem((4,)), sem((7,)), sem((7,)),
             sem((CHUNKS, 32)), sem((CHUNKS, 32)), sem((CHUNKS, 32)), sem((CHUNKS, 32)),
-            sem((3, 3, 4)), sem((3, 3, 4)),
+            sem((3, 3, 10)), sem((3, 3, 10)),
             sem((7,)), sem((7,)), sem((7,)), sem((7,)), sem((7,)), sem((7,)),
             pltpu.VMEM((8, 8, 128), f32), sem((7,)), sem((7,)),
             pltpu.VMEM((8, CHUNKS, SLOTS, 128), f32),

time: 174 us -> 167 us (0.960)
  Pallas kernels: 171 us -> 164 us
    pallas_call x1, Pallas kernels: 171 us -> 164 us  [layer_loss(): pl.pallas_call(expert_body, out_shape=jax.ShapeDtypeStruct((8, 128), f32)...]
where the time goes in v5:
time: 167 us
  Pallas kernels  164 us (98%)
  local copies, waits for them, and re-layouts  2.66 us (2%)
    pallas_call x1, Pallas kernels, layer_loss(): pl.pallas_call(expert_body, out_shape=jax.ShapeDtypeStruct((8, 128), f32)...  164 us

profile of v5, /device:TPU:0, one launch (start us, length us, event | category | flops | bytes accessed | tf_op | source)
XLA Modules:
  0.0 166.7 jit_solution(8044122437090532719)
XLA Ops:
  0.0 1.4 copy.11.weights_ref
  1.4 164.0 %layer_loss.1 = f32[8,128]{1,0:T(8,128)} custom-call(bf16[128,512]{1,0:T(8,128)(2,1)} %tok_ref.1, f32[1,512]{1,0:T(1,128)} %bitcast.9, s32[2,128]{1,0:T(2,128)} %bitcast.11, f32[128,2]{1,0:T(8,128)} %copy.11.weights_ref, f32[1,512]{1,0:T(1,128)} %bitcast.10, s32[8,1,128]{2,1,0:T(1,128)} %bitcast.8, bf16[1,4096,896]{2,1,0:T(8,128)(2,1)} %wg_hbm.1, ...), custom_call_target="tpu_custom_call" | custom-call | tf_op jit(solution)/shard_map/layer_loss/pallas_call | solution.py:557
  165.4 0.7 slice.3
  166.1 0.6 dynamic-slice_bitcast_fusion
